TPU v7x, 256 devices: a whole 4x4x8 slice. The times are simulated.
256 devices in a mesh: expert: 32 (over y, z_lo, core), fsdp: 4 (over x), replica: 2 (over z_hi).
Axes of the slice: x: 4, y: 4, z: 8 (z_hi: 2, z_lo: 4; z = z_hi * 4 + z_lo), core: 2. Of those that a mesh axis runs over, the one named last changes fastest.
Arguments:
- out_grad: bfloat16 [32768, 2048], P(('expert', 'fsdp', 'replica')), may hold values from -6 to 6
- hidden_saved: bfloat16 [32768, 8, 768], P(('expert', 'fsdp', 'replica')), may hold values from -6 to 6
- gate_probs: float32 [32768, 8], P(('expert', 'fsdp', 'replica')), may hold values from 0.05 to 0.5
- expert_ids: int32 [32768, 8], P(('expert', 'fsdp', 'replica')), may hold values from 0 to 63, all different within a row; in each aligned block of 128 rows (0 to 127, 128 to 255, ...) at most 32 rows name the same one
- weight_q: bfloat16 [64, 768, 2048], P('expert', 'fsdp'), may hold values from -0.21875 to 0.21875
- weight_exp: int32 [64, 768, 16], P('expert', 'fsdp'), may hold values from -1 to 1
- master: float32 [64, 768, 2048], P('expert', ('fsdp', 'replica')), may hold values from -0.21875 to 0.21875
- moment1: bfloat16 [64, 768, 2048], P('expert', ('fsdp', 'replica')), may hold values from -6 to 6
- moment2: bfloat16 [64, 768, 2048], P('expert', ('fsdp', 'replica')), may hold values from 0.099609375 to 10
Outputs:
- hidden_grad: bfloat16 [32768, 8, 768], P(('expert', 'fsdp', 'replica'))
- gate_grad: float32 [32768, 8], P(('expert', 'fsdp', 'replica'))
- master_new: float32 [64, 768, 2048], P('expert', ('fsdp', 'replica'))
- moment1_new: bfloat16 [64, 768, 2048], P('expert', ('fsdp', 'replica'))
- moment2_new: bfloat16 [64, 768, 2048], P('expert', ('fsdp', 'replica'))
Inputs may be any that keep to these rules, and one draw needn't show every extreme that they name: `expert_ids`: each token names 8 different experts; the tokens of one device name any one expert at most 32 times.
All inputs are finite; a program needn't handle non-finite values.
Results may differ from a plain program's by a relative error of at most 0.0051.
Values may be sent and summed in bfloat16 or wider, within the bound.
A program may use at most 128 MiB of HBM per device.

v0:
```python
import jax
import jax.numpy as jnp
from jax import lax
from jax.sharding import PartitionSpec as P


def in_one_piece(arrays, axis, split_dim, concat_dim, along):
    both = jnp.concatenate(arrays, axis=along)
    out, at, outs = (
        lax.all_to_all(both, axis, split_axis=split_dim, concat_axis=concat_dim, tiled=True),
        0,
        [],
    )
    for a in arrays:
        outs.append(lax.slice_in_dim(out, at, at + a.shape[along], axis=along))
        at += a.shape[along]
    return tuple(outs)


def cut_along(x, dim, size):
    lengths = x.shape
    parts = x.reshape(*lengths[:dim], size, lengths[dim] // size, *lengths[dim + 1 :])
    return jnp.moveaxis(parts, dim, 0)


def sum_at_owner(x, axis, dim):
    size = lax.axis_size(axis)
    parts = lax.all_to_all(cut_along(x, dim, size), axis, 0, 0, tiled=True)
    return jnp.sum(parts, axis=0)


def body(
    out_grad, hidden_saved, gate_probs, expert_ids, weight_q, weight_exp, master, moment1, moment2
):
    tokens_here, top_count = expert_ids.shape
    experts_here, rows_here, model_width = weight_q.shape
    hidden_width = hidden_saved.shape[2]
    expert_groups = lax.axis_size("expert")
    experts_all = expert_groups * experts_here
    capacity = min(tokens_here, 2 * tokens_here * top_count // experts_all)
    routes = tokens_here * top_count
    flat_ids = expert_ids.reshape(-1)
    onehot = (flat_ids[:, None] == jnp.arange(experts_all, dtype=jnp.int32)[None, :]).astype(
        jnp.int32
    )
    rank_in_expert = jnp.sum(jnp.cumsum(onehot, axis=0) * onehot, axis=1) - 1
    slot_index = flat_ids * capacity + rank_in_expert
    route_of_slot = (
        jnp.full((experts_all * capacity,), routes, jnp.int32)
        .at[slot_index]
        .set(jnp.arange(routes, dtype=jnp.int32))
    )
    filled = route_of_slot < routes
    clamped = jnp.minimum(route_of_slot, routes - 1)
    weighted = (
        (gate_probs[..., None] * hidden_saved.astype(jnp.float32))
        .astype(jnp.bfloat16)
        .reshape(routes, hidden_width)
    )
    zero_value = jnp.zeros((), jnp.bfloat16)
    dy_send = jnp.where(filled[:, None], out_grad[clamped // top_count], zero_value)
    weighted_send = jnp.where(filled[:, None], weighted[clamped], zero_value)
    dy_send = dy_send.reshape(expert_groups, experts_here, capacity, model_width)
    weighted_send = weighted_send.reshape(expert_groups, experts_here, capacity, hidden_width)
    recv_dy, recv_weighted = in_one_piece((dy_send, weighted_send), "expert", 0, 0, 3)
    scales = jnp.exp2(weight_exp.astype(jnp.float32))
    blocks = weight_exp.shape[2]
    weight_local = (
        (
            weight_q.astype(jnp.float32).reshape(
                experts_here, rows_here, blocks, model_width // blocks
            )
            * scales[..., None]
        )
        .reshape(experts_here, rows_here, model_width)
        .astype(jnp.bfloat16)
    )
    back_rows = jnp.einsum(
        "secd,efd->secf",
        recv_dy,
        lax.all_gather(weight_local, "fsdp", axis=1, tiled=True),
        preferred_element_type=jnp.float32,
    ).astype(jnp.bfloat16)
    returned = lax.all_to_all(back_rows, "expert", split_axis=0, concat_axis=0, tiled=True)
    back_route = returned.reshape(experts_all * capacity, hidden_width)[slot_index].reshape(
        tokens_here, top_count, hidden_width
    )
    back_float = back_route.astype(jnp.float32)
    hidden_grad = (gate_probs[..., None] * back_float).astype(jnp.bfloat16)
    gate_grad = jnp.sum(hidden_saved.astype(jnp.float32) * back_float, axis=-1)
    partial_grad = jnp.einsum(
        "secf,secd->efd", recv_weighted, recv_dy, preferred_element_type=jnp.float32
    )
    summed = lax.psum_scatter(partial_grad, "fsdp", scatter_dimension=1, tiled=True)
    gradient = sum_at_owner(summed, "replica", 1)
    first = 0.9 * moment1.astype(jnp.float32) + 0.1 * gradient
    second = 0.95 * moment2.astype(jnp.float32) + 0.05 * gradient * gradient
    update = first / (1.0 - 0.9**20) / (jnp.sqrt(second / (1.0 - 0.95**20)) + 1e-08) + 0.1 * master
    master_new = master - 0.001 * update
    return (
        hidden_grad,
        gate_grad,
        master_new,
        first.astype(jnp.bfloat16),
        second.astype(jnp.bfloat16),
    )


def solution(mesh):
    in_specs = (
        P(("expert", "fsdp", "replica"), None),
        P(("expert", "fsdp", "replica"), None, None),
        P(("expert", "fsdp", "replica"), None),
        P(("expert", "fsdp", "replica"), None),
        P("expert", "fsdp", None),
        P("expert", "fsdp", None),
        P("expert", ("fsdp", "replica"), None),
        P("expert", ("fsdp", "replica"), None),
        P("expert", ("fsdp", "replica"), None),
    )
    out_specs = (
        P(("expert", "fsdp", "replica"), None, None),
        P(("expert", "fsdp", "replica"), None),
        P("expert", ("fsdp", "replica"), None),
        P("expert", ("fsdp", "replica"), None),
        P("expert", ("fsdp", "replica"), None),
    )
    return jax.shard_map(body, mesh=mesh, in_specs=in_specs, out_specs=out_specs, check_vma=False)
```

profile of v0, /device:TPU:32, one launch (start us, length us, event | category | flops | bytes accessed | tf_op | source)
XLA Modules:
  0.0 563.3 jit_solution(7500704694192222670)
XLA Ops:
  8.9 18.0 %reduce-window.6 = s32[64,8,128]{2,1,0:T(8,128)S(1)} reduce-window(s32[64,8,128]{2,1,0:T(8,128)S(1)} %fusion.22, s32[]{:T(128)} %constant.24.clone.1), window={size=1x1x128 pad=0_0x0_0x127_0}, to_apply=%region_0.0 | reduce-window | flops 8323072 | bytes 524292 | tf_op jit(solution)/shard_map/reduce-window
  27.8 4.3 scatter_custom_fusion
  33.0 1.7 fusion.17
  34.8 9.4 %gather_fusion.1 = bf16[2048,768]{1,0:T(8,128)(2,1)} fusion(bf16[1024,768]{1,0:T(8,128)(2,1)S(1)} %fusion.17, s32[2048]{0:T(1024)S(1)} %get-tuple-element.16), kind=kCustom, calls=%fused_computation.1 | custom fusion | bytes 6299648 | tf_op jit(solution)/shard_map/gather | solution.py:62
  44.2 3.4 broadcast_select_fusion.1
  47.6 11.0 %gather_fusion = bf16[2048,2048]{1,0:T(8,128)(2,1)} fusion(bf16[128,2048]{1,0:T(8,128)(2,1)S(1)} %copy-done, s32[2048]{0:T(1024)S(1)} %get-tuple-element.15), kind=kCustom, calls=%fused_computation | custom fusion | bytes 16785408 | tf_op jit(solution)/shard_map/gather | solution.py:61
  58.6 7.5 %broadcast_select_fusion = bf16[32,2,32,2048]{3,2,1,0:T(8,128)(2,1)} fusion(bf16[32,2,32,2048]{3,2,1,0:T(8,128)(2,1)} %bitcast.44, pred[32,2,32]{2,1,0:T(4,128)(4,1)S(1)} %broadcast_in_dim.40), kind=kLoop, calls=%fused_computation.5 | loop fusion | flops 4194304 | bytes 16779264 | tf_op jit(solution)/shard_map/jit(_where)/select_n | solution.py:61
  66.0 9.0 %pad_maximum_fusion = bf16[32,2,32,2816]{3,2,1,0:T(8,128)(2,1)} fusion(bf16[32,2,32,768]{3,2,1,0:T(8,128)(2,1)S(1)} %copy-done.2, bf16[32,2,32,2048]{3,2,1,0:T(8,128)(2,1)} %broadcast_select_fusion), kind=kLoop, calls=%fused_computation.4 | loop fusion | flops 23068672 | bytes 23068672 | tf_op jit(solution)/shard_map/concatenate | solution.py:8
  75.0 9.0 %all-to-all-start = ((bf16[32,2,32,2816]{3,2,1,0:T(8,128)(2,1)}), bf16[32,2,32,2816]{3,2,1,0:T(8,128)(2,1)}, u32[]{:S(2)}, u32[]{:S(2)}) async-start(bf16[32,2,32,2816]{3,2,1,0:T(8,128)(2,1)} %pad_maximum_fusion), calls=%async_computation | async-start | bytes 23068672 | tf_op jit(solution)/shard_map/all_to_all | solution.py:10
  85.1 2.3 mul.82
  87.3 4.0 multiply_convert_fusion
  91.6 240.1 %all-to-all-done = bf16[32,2,32,2816]{3,2,1,0:T(8,128)(2,1)} async-done(((bf16[32,2,32,2816]{3,2,1,0:T(8,128)(2,1)}), bf16[32,2,32,2816]{3,2,1,0:T(8,128)(2,1)}, u32[]{:S(2)}, u32[]{:S(2)}) %all-to-all-start) | async-done | bytes 11534368 | tf_op jit(solution)/shard_map/all_to_all | solution.py:10
  331.7 13.5 %fusion.5 = f32[2,768,2048]{2,1,0:T(8,128)} fusion(bf16[32,2,32,2816]{3,2,1,0:T(8,128)(2,1)} %all-to-all-done), kind=kOutput, calls=%fused_computation.11 | convolution fusion | flops 6442450944 | bytes 24117248 | tf_op jit(solution)/shard_map/secf,secd->efd/dot_general | solution.py:91
  345.3 11.0 %convert_bitcast_fusion = bf16[32,2,32,768]{3,2,0,1:T(8,128)(2,1)S(1)} fusion(bf16[2,768,2048]{2,1,0:T(8,128)(2,1)} %all-gather.2.cloned.1.call-done, bf16[32,2,32,2816]{3,2,1,0:T(8,128)(2,1)} %all-to-all-done), kind=kOutput, calls=%fused_computation.20 | convolution fusion | flops 6444023808 | bytes 17825792 | tf_op jit(solution)/shard_map/secd,efd->secf/dot_general | solution.py:78
  356.2 1.9 copy.40
  358.1 8.9 %all-to-all-start.1 = ((bf16[32,2,32,768]{3,2,1,0:T(8,128)(2,1)}), bf16[32,2,32,768]{3,2,1,0:T(8,128)(2,1)S(1)}, u32[]{:S(2)}, u32[]{:S(2)}) async-start(bf16[32,2,32,768]{3,2,1,0:T(8,128)(2,1)} %copy.40), calls=%async_computation.1 | async-start | bytes 6291456 | tf_op jit(solution)/shard_map/all_to_all | solution.py:84
  367.0 98.7 %reduce-scatter.2.cloned.1.call-done = f32[2,192,2048]{2,1,0:T(8,128)} async-done(((f32[2,768,2048]{2,1,0:T(8,128)}), f32[2,192,2048]{2,1,0:T(8,128)}) %reduce-scatter.2.cloned.1.call-update) | async-done | bytes 3145744 | tf_op jit(solution)/shard_map/reduce_scatter | solution.py:94
  465.7 3.9 copy.61
  469.6 6.1 %all-to-all-start.2 = ((f32[2,2,96,2048]{3,2,1,0:T(8,128)}), f32[2,2,96,2048]{3,2,1,0:T(8,128)}, u32[]{:S(2)}, u32[]{:S(2)}) async-start(f32[2,2,96,2048]{3,2,1,0:T(8,128)} %bitcast.45), calls=%async_computation.3 | async-start | bytes 6291456 | tf_op jit(solution)/shard_map/all_to_all | solution.py:28
  475.7 5.2 gather_fusion.2
  480.9 3.9 fusion.10
  485.5 63.5 %all-to-all-done.2 = f32[2,2,96,2048]{3,2,1,0:T(8,128)} async-done(((f32[2,2,96,2048]{3,2,1,0:T(8,128)}), f32[2,2,96,2048]{3,2,1,0:T(8,128)}, u32[]{:S(2)}, u32[]{:S(2)}) %all-to-all-start.2) | async-done | bytes 3145760 | tf_op jit(solution)/shard_map/all_to_all | solution.py:28
  549.0 2.3 reduce_sum.29
  551.3 5.1 fusion.19
  (42 shorter events, 5.4 us)
Async XLA Ops:
  7.2 40.4 %copy-start = (bf16[128,2048]{1,0:T(8,128)(2,1)S(1)}, bf16[128,2048]{1,0:T(8,128)(2,1)}, u32[]{:S(2)}) copy-start(bf16[128,2048]{1,0:T(8,128)(2,1)} %param.9) | copy-start | bytes 1572868
  58.6 7.5 %copy-start.2 = (bf16[32,2,32,768]{3,2,1,0:T(8,128)(2,1)S(1)}, bf16[32,2,32,768]{3,2,1,0:T(8,128)(2,1)}, u32[]{:S(2)}) copy-start(bf16[32,2,32,768]{3,2,1,0:T(8,128)(2,1)} %broadcast_select_fusion.1) | copy-start | bytes 9437188
  75.0 9.0 %copy-start.4 = (s32[2,192,16]{1,2,0:T(8,128)S(1)}, s32[2,192,16]{1,2,0:T(8,128)}, u32[]{:S(2)}) copy-start(s32[2,192,16]{1,2,0:T(8,128)} %param.14) | copy-start | bytes 73732
  75.0 256.7 %all-to-all-start = ((bf16[32,2,32,2816]{3,2,1,0:T(8,128)(2,1)}), bf16[32,2,32,2816]{3,2,1,0:T(8,128)(2,1)}, u32[]{:S(2)}, u32[]{:S(2)}) async-start(bf16[32,2,32,2816]{3,2,1,0:T(8,128)(2,1)} %pad_maximum_fusion), calls=%async_computation | async-start | bytes 23068672 | tf_op jit(solution)/shard_map/all_to_all | solution.py:10
  84.0 261.3 %all-gather.2.cloned.1.call-start = ((), (), s32[]{:S(2)}) async-start(), calls=%async_computation.4 | async-start | bytes 7864320 | tf_op jit(solution)/shard_map/all_gather | solution.py:81
  91.4 374.3 %reduce-scatter.2.cloned.1.call-start = ((), (), s32[]{:S(2)}) async-start(), calls=%async_computation.5 | async-start | bytes 15728640 | tf_op jit(solution)/shard_map/reduce_scatter | solution.py:94
  358.1 111.5 %all-to-all-start.1 = ((bf16[32,2,32,768]{3,2,1,0:T(8,128)(2,1)}), bf16[32,2,32,768]{3,2,1,0:T(8,128)(2,1)S(1)}, u32[]{:S(2)}, u32[]{:S(2)}) async-start(bf16[32,2,32,768]{3,2,1,0:T(8,128)(2,1)} %copy.40), calls=%async_computation.1 | async-start | bytes 6291456 | tf_op jit(solution)/shard_map/all_to_all | solution.py:84
  469.6 79.4 %all-to-all-start.2 = ((f32[2,2,96,2048]{3,2,1,0:T(8,128)}), f32[2,2,96,2048]{3,2,1,0:T(8,128)}, u32[]{:S(2)}, u32[]{:S(2)}) async-start(f32[2,2,96,2048]{3,2,1,0:T(8,128)} %bitcast.45), calls=%async_computation.3 | async-start | bytes 6291456 | tf_op jit(solution)/shard_map/all_to_all | solution.py:28
  484.8 66.5 %copy-start.3 = (bf16[2,96,2048]{2,1,0:T(8,128)(2,1)S(1)}, bf16[2,96,2048]{2,1,0:T(8,128)(2,1)}, u32[]{:S(2)}) copy-start(bf16[2,96,2048]{2,1,0:T(8,128)(2,1)} %param.17) | copy-start | bytes 2359300
  549.0 7.4 %copy-start.1 = (bf16[128,2048]{1,0:T(8,128)(2,1)S(1)}, bf16[128,2048]{1,0:T(8,128)(2,1)}, u32[]{:S(2)}) copy-start(bf16[128,2048]{1,0:T(8,128)(2,1)} %param.9) | copy-start | bytes 1572868
Sparse Core Ops, SparseCore 0:
  91.5 68.3 all-gather.1
  345.3 120.3 reduce-scatter.1
where the time goes:
time: 565 us; the launch traced here: 563 us
  waiting for transfers between devices  402 us (71%)
  other arithmetic  55.8 us (10%)
  local copies, waits for them, and re-layouts  42.1 us (7%)
  matrix products  24.5 us (4%)
  starting transfers between devices  24.3 us (4%)
  between operations  14.2 us (3%)
    all_to_all x1, waiting for transfers between devices, in_one_piece(): lax.all_to_all(both, axis, split_axis=split_dim, concat_axis=concat_dim,...  240 us
    reduce_scatter x1, waiting for transfers between devices, body(): lax.psum_scatter(partial_grad, 'fsdp', scatter_dimension=1, tiled=True)  98.7 us
    all_to_all x1, waiting for transfers between devices, sum_at_owner(): parts = lax.all_to_all(cut_along(x, dim, size), axis, 0, 0, tiled=True)  63.5 us
    another operation x3, other arithmetic  18.2 us
    dot_general x1, matrix products, body(): jnp.einsum('secf,secd->efd', recv_weighted, recv_dy, preferred_element_ty...  13.5 us
  transfers between devices with their start and end apart: 5, of which 3 were waited for; matrix products, arithmetic and copies ran while one was open for 8% of the time, Pallas kernels for 0%

commit v1 on v0

v1 whole, which is shorter than its diff:
```python
import jax
import jax.numpy as jnp
from jax import lax
from jax.experimental import pallas as pl
from jax.experimental.pallas import tpu as pltpu
from jax.sharding import PartitionSpec as P

MESH = pl.DeviceIdType.MESH
NY, NZ, NZL, NX = 4, 8, 4, 4
CAP = 32
ANY = pl.BlockSpec(memory_space=pl.ANY)
VMEM = pl.BlockSpec(memory_space=pltpu.VMEM)


class Place:
    def __init__(self):
        self.own = lax.axis_index("expert")
        self.core = lax.rem(self.own, 2)
        self.y = self.own // (2 * NZL)
        self.z = lax.axis_index("replica") * NZL + lax.rem(self.own // 2, NZL)
        self.x = lax.axis_index("fsdp")
        self.s = 1 - 2 * self.core

    def slot(self, dy, dz, core):
        y = lax.rem(self.y + dy + NY, NY)
        zl = lax.rem(self.z + dz + NZ, NZL)
        return (y * NZL + zl) * 2 + core

    def dev(self, dy, dz, core):
        return {
            "expert": self.slot(dy, dz, core),
            "replica": lax.rem(self.z + dz + NZ, NZ) // NZL,
        }

    def dev_x(self, dx):
        return {"fsdp": lax.rem(self.x + dx + NX, NX)}


def remote(src, dst, ssem, rsem, dev):
    return pltpu.make_async_remote_copy(
        src_ref=src, dst_ref=dst, send_sem=ssem, recv_sem=rsem, device_id=dev, device_id_type=MESH
    )


def peers(p, far):
    out = []
    for dc in (0, 1):
        core = p.core if dc == 0 else 1 - p.core
        for dy in range(NY):
            for kind in range(NZL):
                if dc == 0 and dy == 0 and kind == 0:
                    continue
                dz = (0, 1, far(core), -1)[kind]
                out.append(p.dev(dy, dz, core))
    return out


def dispatch_kernel(
    dy_ref, ws_ref, code_ref, w_ref, rdy_ref, rw_ref, rcode_ref, wf_ref,
    dy_ss, dy_rs, b_ss, b_rs, c_ss, c_rs, w_ss, w_rs, l_sem,
):
    p = Place()
    core, s = p.core, p.s
    half = dy_ref.shape[0] // 2
    sends = []
    count = [0, 0]

    def start(c):
        c.start()
        sends.append(c)

    def part(slot, h):
        return rdy_ref.at[slot, pl.ds(h * half, half)]

    def at(h, a, b):
        return (a, b) if h == 0 else (b, a)

    def send_dy(src, slot, h, dev):
        k = count[h]
        count[h] += 1
        start(remote(src, part(slot, h), dy_ss.at[h, k], dy_rs.at[h, slot], dev))

    def wait_dy(slot, h):
        blk = part(slot, h)
        remote(blk, blk, dy_ss.at[h, 0], dy_rs.at[h, slot], p.dev(1, 0, core)).wait_recv()

    local = [
        pltpu.make_async_copy(w_ref, wf_ref.at[p.x], l_sem.at[0]),
        pltpu.make_async_copy(dy_ref, rdy_ref.at[p.own], l_sem.at[1]),
        pltpu.make_async_copy(ws_ref.at[p.own], rw_ref.at[p.own], l_sem.at[2]),
        pltpu.make_async_copy(code_ref.at[p.own], rcode_ref.at[p.own], l_sem.at[3]),
    ]
    for c in local:
        c.start()

    for i, dx in enumerate((1, -1)):
        start(remote(w_ref, wf_ref.at[p.x], w_ss.at[i], w_rs.at[p.x], p.dev_x(dx)))

    def mine(h):
        return dy_ref.at[pl.ds(h * half, half)]

    for h in (0, 1):
        for d in (1, -1):
            send_dy(mine(h), p.own, h, p.dev(*at(h, d, 0), core))
    for h in (0, 1):
        for d in (1, -1):
            send_dy(mine(h), p.own, h, p.dev(*at(h, 0, d), core))
        send_dy(mine(h), p.own, h, p.dev(0, 0, 1 - core))

    for k, dev in enumerate(peers(p, lambda c: 2 * s)):
        tgt = dev["expert"]
        start(remote(ws_ref.at[tgt], rw_ref.at[p.own], b_ss.at[k], b_rs.at[p.own], dev))
        start(remote(code_ref.at[tgt], rcode_ref.at[p.own], c_ss.at[k], c_rs.at[p.own], dev))

    for h in (0, 1):
        b = p.slot(*at(h, -s, 0), core)
        wait_dy(b, h)
        send_dy(part(b, h), b, h, p.dev(*at(h, s, 0), core))

    for i, a in enumerate((-s, s, -2 * s)):
        for h in (0, 1):
            b = p.slot(*at(h, a, 0), core)
            if i > 0:
                wait_dy(b, h)
            for d in (1, -1):
                send_dy(part(b, h), b, h, p.dev(*at(h, 0, d), core))
            send_dy(part(b, h), b, h, p.dev(0, 0, 1 - core))

    back_x = lax.rem(p.x - s + NX, NX)
    shard = wf_ref.at[back_x]
    remote(shard, shard, w_ss.at[2], w_rs.at[back_x], p.dev_x(s)).wait_recv()
    start(remote(shard, shard, w_ss.at[2], w_rs.at[back_x], p.dev_x(s)))

    for a in (0, -s, s, -2 * s):
        for h in (0, 1):
            b = p.slot(*at(h, a, -s), core)
            wait_dy(b, h)
            send_dy(part(b, h), b, h, p.dev(*at(h, 0, s), core))
            send_dy(part(b, h), b, h, p.dev(0, 0, 1 - core))
    for d in (s, -2 * s):
        for a in (0, -s, s, -2 * s):
            for h in (0, 1):
                b = p.slot(*at(h, a, d), core)
                wait_dy(b, h)
                send_dy(part(b, h), b, h, p.dev(0, 0, 1 - core))

    for dx in (1, 2):
        j = lax.rem(p.x + dx * s + NX + NX, NX)
        blk = wf_ref.at[j]
        remote(blk, blk, w_ss.at[0], w_rs.at[j], p.dev_x(1)).wait_recv()
    for dc in (0, 1):
        c2 = core if dc == 0 else 1 - core
        for dy in range(NY):
            for dz in range(NZL):
                j = p.slot(dy, dz, c2)
                if dc == 1:
                    for h in (0, 1):
                        wait_dy(j, h)
                elif dy == 0 and dz == 0:
                    continue
                a, b = rw_ref.at[j], rcode_ref.at[j]
                remote(a, a, b_ss.at[0], b_rs.at[j], p.dev(1, 0, core)).wait_recv()
                remote(b, b, c_ss.at[0], c_rs.at[j], p.dev(1, 0, core)).wait_recv()
    for c in local:
        c.wait()
    for c in sends:
        c.wait_send()


def dispatch(dy, ws, code, w):
    n, e2c, f = ws.shape
    bf = jnp.bfloat16
    dma = pltpu.SemaphoreType.DMA
    return pl.pallas_call(
        dispatch_kernel,
        out_shape=(
            jax.ShapeDtypeStruct((n,) + dy.shape, bf),
            jax.ShapeDtypeStruct(ws.shape, bf),
            jax.ShapeDtypeStruct(code.shape, jnp.float32),
            jax.ShapeDtypeStruct((NX,) + w.shape, bf),
        ),
        in_specs=[VMEM, ANY, ANY, VMEM],
        out_specs=(ANY, ANY, ANY, ANY),
        scratch_shapes=[
            dma((2, 31)), dma((2, 32)), dma((31,)), dma((32,)), dma((31,)), dma((32,)),
            dma((3,)), dma((4,)), dma((4,)),
        ],
        compiler_params=pltpu.CompilerParams(has_side_effects=True),
        name="dispatch",
    )(dy, ws, code, w)


def giveback_kernel(back_ref, grad_ref, rb_ref, rg_ref, d_ss, d_rs, e_ss, e_rs, l_sem):
    p = Place()
    core = p.core
    sends = []

    def start(c):
        c.start()
        sends.append(c)

    local = [
        pltpu.make_async_copy(back_ref.at[p.own], rb_ref.at[p.own], l_sem.at[0]),
    ]
    for c in local:
        c.start()
    for k, dev in enumerate(peers(p, lambda c: 4 * c - 2)):
        src = back_ref.at[dev["expert"]]
        start(remote(src, rb_ref.at[p.own], d_ss.at[k], d_rs.at[p.own], dev))
    for k, dx in enumerate((1, -1, 2)):
        tgt = lax.rem(p.x + dx + NX, NX)
        start(remote(grad_ref.at[tgt], rg_ref.at[k], e_ss.at[k], e_rs.at[k], p.dev_x(dx)))
    for dc in (0, 1):
        c2 = core if dc == 0 else 1 - core
        for dy in range(NY):
            for dz in range(NZL):
                if dc == 0 and dy == 0 and dz == 0:
                    continue
                j = p.slot(dy, dz, c2)
                a = rb_ref.at[j]
                remote(a, a, d_ss.at[0], d_rs.at[j], p.dev(1, 0, core)).wait_recv()
    for k in range(3):
        a = rg_ref.at[k]
        remote(a, a, e_ss.at[k], e_rs.at[k], p.dev_x(1)).wait_recv()
    for c in local:
        c.wait()
    for c in sends:
        c.wait_send()


def giveback(back, grad):
    dma = pltpu.SemaphoreType.DMA
    bf = jnp.bfloat16
    return pl.pallas_call(
        giveback_kernel,
        out_shape=(
            jax.ShapeDtypeStruct(back.shape, bf),
            jax.ShapeDtypeStruct((NX - 1,) + grad.shape[1:], bf),
        ),
        in_specs=[ANY, ANY],
        out_specs=(ANY, ANY),
        scratch_shapes=[dma((31,)), dma((32,)), dma((3,)), dma((3,)), dma((1,))],
        compiler_params=pltpu.CompilerParams(has_side_effects=True),
        name="giveback",
    )(back, grad)


def prep_kernel(ids_ref, ids_t_ref, w_ref, ws_ref, code_ref, slot_ref):
    experts = code_ref.shape[0]
    routes = ids_ref.shape[1]
    tokens = ids_t_ref.shape[1]
    f32, bf = jnp.float32, jnp.bfloat16

    def ranks(named, n):
        before = lax.broadcasted_iota(jnp.int32, (n, n), 0) < lax.broadcasted_iota(
            jnp.int32, (n, n), 1
        )
        return jnp.dot(named.astype(bf), before.astype(bf), preferred_element_type=f32)

    ids = ids_ref[...]
    named = jnp.where(
        ids == lax.broadcasted_iota(jnp.int32, (experts, routes), 0), 1.0, 0.0
    ).astype(f32)
    rank = jnp.sum(named * ranks(named, routes), axis=0, keepdims=True)
    slot = ids * CAP + rank.astype(jnp.int32)
    slot_ref[...] = slot

    ids_t = ids_t_ref[...]
    named_t = jnp.zeros((experts, tokens), f32)
    for k in range(ids_t_ref.shape[0]):
        named_t += jnp.where(
            ids_t[k : k + 1] == lax.broadcasted_iota(jnp.int32, (experts, tokens), 0), 1.0, 0.0
        )
    code_ref[...] = jnp.where(named_t > 0, ranks(named_t, tokens), -1.0)

    step = 256

    def body(i, _):
        at = pl.multiple_of(i * step, step)
        pick = (slot == lax.broadcasted_iota(jnp.int32, (step, routes), 0) + at).astype(f32)
        ws_ref[pl.ds(at, step)] = jnp.dot(
            pick.astype(bf), w_ref[...], preferred_element_type=f32
        ).astype(bf)
        return 0

    lax.fori_loop(0, ws_ref.shape[0] // step, body, 0)


def prep(ids, ids_t, weighted, experts):
    return pl.pallas_call(
        prep_kernel,
        out_shape=(
            jax.ShapeDtypeStruct((experts * CAP, weighted.shape[1]), jnp.bfloat16),
            jax.ShapeDtypeStruct((experts, ids_t.shape[1]), jnp.float32),
            jax.ShapeDtypeStruct(ids.shape, jnp.int32),
        ),
        in_specs=[VMEM, VMEM, VMEM],
        out_specs=(VMEM, VMEM, VMEM),
        name="prep",
    )(ids, ids_t, weighted)


def combine_kernel(slot_ref, gate_ref, h_ref, rb_ref, hg_ref, gg_ref):
    f32, bf = jnp.float32, jnp.bfloat16
    rows, slots = slot_ref.shape[0], rb_ref.shape[0]
    pick = (slot_ref[...] == lax.broadcasted_iota(jnp.int32, (rows, slots), 1)).astype(f32)
    back = jnp.dot(pick.astype(bf), rb_ref[...], preferred_element_type=f32)
    hg_ref[...] = (gate_ref[...] * back).astype(bf)
    gg_ref[...] = jnp.sum(h_ref[...].astype(f32) * back, axis=1, keepdims=True)


def combine(slot, gate, hidden, returned):
    routes, f = hidden.shape
    step = 256
    return pl.pallas_call(
        combine_kernel,
        grid=(routes // step,),
        out_shape=(
            jax.ShapeDtypeStruct((routes, f), jnp.bfloat16),
            jax.ShapeDtypeStruct((routes, 1), jnp.float32),
        ),
        in_specs=[
            pl.BlockSpec((step, 1), lambda i: (i, 0)),
            pl.BlockSpec((step, 1), lambda i: (i, 0)),
            pl.BlockSpec((step, f), lambda i: (i, 0)),
            pl.BlockSpec(returned.shape, lambda i: (0, 0)),
        ],
        out_specs=(
            pl.BlockSpec((step, f), lambda i: (i, 0)),
            pl.BlockSpec((step, 1), lambda i: (i, 0)),
        ),
        name="combine",
    )(slot, gate, hidden, returned)


def body(
    out_grad, hidden_saved, gate_probs, expert_ids, weight_q, weight_exp, master, moment1, moment2
):
    f32, bf = jnp.float32, jnp.bfloat16
    tokens, top = expert_ids.shape
    held, rows, width = weight_q.shape
    hid = hidden_saved.shape[2]
    groups = lax.axis_size("expert")
    experts = groups * held
    routes = tokens * top

    gate_col = gate_probs.reshape(routes, 1)
    hidden = hidden_saved.reshape(routes, hid)
    weighted = (gate_probs[..., None] * hidden_saved.astype(f32)).astype(bf).reshape(routes, hid)
    ids = expert_ids.reshape(1, routes)
    sent, code, slot = prep(ids, expert_ids.T, weighted, experts)

    scales = jnp.exp2(weight_exp.astype(f32))
    blocks = weight_exp.shape[2]
    weight = (
        (weight_q.astype(f32).reshape(held, rows, blocks, width // blocks) * scales[..., None])
        .reshape(held, rows, width)
        .astype(bf)
    )
    r_dy, r_w, r_code, w_full = dispatch(
        out_grad,
        sent.reshape(groups, held * CAP, hid),
        code.reshape(groups, held, tokens),
        weight,
    )
    pick = (
        r_code[:, :, None, :] == jnp.arange(CAP, dtype=f32)[None, None, :, None]
    ).astype(bf).reshape(groups, held * CAP, tokens)
    rows_dy = jnp.einsum("sct,std->scd", pick, r_dy, preferred_element_type=f32).astype(bf)
    rows_dy = rows_dy.reshape(groups, held, CAP, width)
    rows_w = r_w.reshape(groups, held, CAP, hid)
    back = jnp.einsum(
        "secd,xefd->secxf", rows_dy, w_full, preferred_element_type=f32
    ).astype(bf)
    grad = jnp.einsum(
        "secxf,secd->xefd",
        rows_w.reshape(groups, held, CAP, NX, rows),
        rows_dy,
        preferred_element_type=f32,
    )
    r_back, r_grad = giveback(back.reshape(groups, held * CAP, hid), grad.astype(bf))
    hidden_grad, gate_grad = combine(
        slot.reshape(routes, 1), gate_col, hidden, r_back.reshape(experts * CAP, hid)
    )

    own = lax.dynamic_index_in_dim(grad, lax.axis_index("fsdp"), 0, keepdims=False)
    summed = own + jnp.sum(r_grad.astype(f32), axis=0)
    summed = summed.reshape(held, 2, rows // 2, width)
    me = lax.axis_index("replica")
    other = lax.dynamic_index_in_dim(summed, 1 - me, 1, keepdims=False)
    got = lax.ppermute(other.astype(bf), "replica", [(0, 1), (1, 0)])
    gradient = lax.dynamic_index_in_dim(summed, me, 1, keepdims=False) + got.astype(f32)

    first = 0.9 * moment1.astype(f32) + 0.1 * gradient
    second = 0.95 * moment2.astype(f32) + 0.05 * gradient * gradient
    update = first / (1.0 - 0.9**20) / (jnp.sqrt(second / (1.0 - 0.95**20)) + 1e-08) + 0.1 * master
    return (
        hidden_grad.reshape(tokens, top, hid),
        gate_grad.reshape(tokens, top),
        master - 0.001 * update,
        first.astype(bf),
        second.astype(bf),
    )


def solution(mesh):
    tok = ("expert", "fsdp", "replica")
    in_specs = (
        P(tok, None),
        P(tok, None, None),
        P(tok, None),
        P(tok, None),
        P("expert", "fsdp", None),
        P("expert", "fsdp", None),
        P("expert", ("fsdp", "replica"), None),
        P("expert", ("fsdp", "replica"), None),
        P("expert", ("fsdp", "replica"), None),
    )
    out_specs = (
        P(tok, None, None),
        P(tok, None),
        P("expert", ("fsdp", "replica"), None),
        P("expert", ("fsdp", "replica"), None),
        P("expert", ("fsdp", "replica"), None),
    )
    return jax.shard_map(body, mesh=mesh, in_specs=in_specs, out_specs=out_specs, check_vma=False)
```

time: 565 us -> 336 us (0.59)
  waiting for transfers between devices: 402 us -> 23 us
  Pallas kernels: 0 us -> 200 us
  other arithmetic: 55.8 us -> 22.5 us
  starting transfers between devices: 24.3 us -> 5.55 us
  between operations: 14.2 us -> 0.72 us
  matrix products: 24.5 us -> 37.7 us
    all_to_all x3 -> x0, waiting for transfers between devices: 304 us -> none  [the longest x1 240 us: in_one_piece(): lax.all_to_all(both, axis, split_axis=split_dim, concat_axis=concat_dim,...]
    pallas_call x0 -> x4, Pallas kernels: none -> 200 us  [the longest x1 102 us: dispatch(): pl.pallas_call(dispatch_kernel, out_shape=(jax.ShapeDtypeStruct((n,) + dy...]
    reduce_scatter x1 -> x0, waiting for transfers between devices: 98.7 us -> none  [body(): lax.psum_scatter(partial_grad, 'fsdp', scatter_dimension=1, tiled=True)]
    gather x3 -> x0, local copies, waits for them, and re-layouts: 25.6 us -> none  [the longest x1 11 us: body(): out_grad[clamped // top_count]]
    all_to_all x3 -> x0, starting transfers between devices: 24 us -> none  [the longest x1 8.97 us: in_one_piece(): lax.all_to_all(both, axis, split_axis=split_dim, concat_axis=concat_dim,...]
    ppermute x0 -> x1, waiting for transfers between devices: none -> 23 us  [body(): got = lax.ppermute(other.astype(bf), 'replica', [(0, 1), (1, 0)])]
    another operation x3 -> x0, other arithmetic: 18.2 us -> none
    dot_general x2 -> x3, matrix products: 24.5 us -> 37.7 us  [the longest x1 13.3 us: body(): jnp.einsum('secd,xefd->secxf', rows_dy, w_full, preferred_element_type=f32)]
  transfers between devices with their start and end apart: 5 -> 1, of which waited for: 3 -> 1; matrix products, arithmetic and copies ran while one was open for 8% -> 1% of each run, Pallas kernels for 0% -> 2%
where the time goes in v1:
time: 336 us
  Pallas kernels  200 us (60%)
  local copies, waits for them, and re-layouts  46.2 us (14%)
  matrix products  37.7 us (11%)
  waiting for transfers between devices  23 us (7%)
  other arithmetic  22.5 us (7%)
  starting transfers between devices  5.55 us (2%)
    pallas_call x1, Pallas kernels, dispatch(): pl.pallas_call(dispatch_kernel, out_shape=(jax.ShapeDtypeStruct((n,) + dy...  102 us
    pallas_call x1, Pallas kernels, giveback(): pl.pallas_call(giveback_kernel, out_shape=(jax.ShapeDtypeStruct(back.shap...  82 us
    ppermute x1, waiting for transfers between devices, body(): got = lax.ppermute(other.astype(bf), 'replica', [(0, 1), (1, 0)])  23 us
    dot_general x1, matrix products, body(): jnp.einsum('secd,xefd->secxf', rows_dy, w_full, preferred_element_type=f32)  13.3 us
    dot_general x1, matrix products, body(): jnp.einsum('secxf,secd->xefd', rows_w.reshape(groups, held, CAP, NX, rows...  13.1 us
    dot_general x1, matrix products, body(): jnp.einsum('sct,std->scd', pick, r_dy, preferred_element_type=f32)  11.3 us
    convert_element_type x1, local copies, waits for them, and re-layouts, body(): back = jnp.einsum('secd,xefd->secxf', rows_dy, w_full, preferred_element_...  10.2 us
    reshape x1, local copies, waits for them, and re-layouts, body(): back.reshape(groups, held * CAP, hid)  8.4 us
  transfers between devices with their start and end apart: 1, of which 1 were waited for; matrix products, arithmetic and copies ran while one was open for 1% of the time, Pallas kernels for 2%

profile of v1, /device:TPU:32, one launch (start us, length us, event | category | flops | bytes accessed | tf_op | source)
XLA Modules:
  0.0 335.6 jit_solution(10406186952681102105)
XLA Ops:
  3.9 2.1 mul.54
  6.0 2.8 mul.55
  8.9 3.0 fusion.15.w_ref
  11.9 1.7 multiply_convert_fusion.w_ref
  13.5 8.1 %prep.1 = (bf16[2048,768]{1,0:T(8,128)(2,1)}, f32[64,128]{1,0:T(8,128)}, s32[1,1024]{1,0:T(1,128)}) custom-call(s32[1,1024]{1,0:T(1,128)} %reshape.59.ids_ref, s32[8,128]{1,0:T(8,128)} %bitcast.60, bf16[1024,768]{1,0:T(8,128)(2,1)} %fusion.15.w_ref), custom_call_target="tpu_custom_call" | custom-call | tf_op jit(solution)/shard_map/prep/pallas_call | solution.py:290
  21.7 102.0 %dispatch.1 = (bf16[32,128,2048]{2,1,0:T(8,128)(2,1)}, bf16[32,64,768]{2,1,0:T(8,128)(2,1)}, f32[32,2,128]{2,1,0:T(2,128)}, bf16[4,2,192,2048]{3,2,1,0:T(8,128)(2,1)}) custom-call(bf16[128,2048]{1,0:T(8,128)(2,1)} %dy_ref.1, bf16[32,64,768]{2,1,0:T(8,128)(2,1)} %bitcast.57, f32[32,2,128]{2,1,0:T(2,128)} %bitcast.59, ...), custom_call_target="tpu_custom_call" | custom-call | tf_op jit(solution)/shard_map/dispatch/pallas_call | solution.py:174
  124.7 11.3 %convolution_convert_fusion = bf16[32,64,2048]{2,1,0:T(8,128)(2,1)} fusion(pred[32,64,128]{2,1,0:T(32,128)(4,1)S(1)} %bitcast_compare_fusion, bf16[32,128,2048]{2,1,0:T(8,128)(2,1)} %get-tuple-element.21), kind=kOutput, calls=%fused_computation.9 | convolution fusion | flops 1077936128 | bytes 25427968 | tf_op jit(solution)/shard_map/sct,std->scd/dot_general | solution.py:369
  136.0 13.3 %convert_bitcast_fusion = bf16[32,2,32,4,192]{4,2,0,3,1:T(8,128)(2,1)S(1)} fusion(bf16[32,2,32,2048,1]{3,2,1,0,4:T(8,128)(2,1)} %bitcast.52, bf16[4,2,192,2048]{3,2,1,0:T(8,128)(2,1)} %get-tuple-element.19), kind=kOutput, calls=%fused_computation.11 | convolution fusion | flops 6444023808 | bytes 17825792 | tf_op jit(solution)/shard_map/secd,xefd->secxf/dot_general | solution.py:372
  149.3 10.2 %copy.32 = bf16[32,2,32,4,192]{4,3,2,1,0:T(4,128)(2,1)} copy(bf16[32,2,32,4,192]{4,2,0,3,1:T(8,128)(2,1)S(1)} %convert_bitcast_fusion) | data formatting | bytes 6291456 | tf_op jit(solution)/shard_map/convert_element_type | solution.py:374
  159.6 8.4 %reshape.67.back_ref = bf16[32,64,768]{2,1,0:T(8,128)(2,1)} reshape(bf16[32,2,32,4,192]{4,3,2,1,0:T(4,128)(2,1)} %copy.32) | data formatting | bytes 6291456 | tf_op jit(solution)/shard_map/reshape | solution.py:381
  168.0 4.7 %reshape_reshape.3 = bf16[32,2,32,4,192]{4,3,2,1,0:T(4,128)(2,1)} reshape(bf16[32,64,768]{2,1,0:T(8,128)(2,1)S(1)} %copy-done.1) | data formatting | bytes 6291456 | tf_op jit(solution)/shard_map/reshape;reshape | solution.py:377
  172.7 13.1 %fusion.6 = f32[2,2048,4,192]{1,3,2,0:T(8,128)} fusion(bf16[32,2,32,2048,1]{3,2,1,0,4:T(8,128)(2,1)} %bitcast.53, bf16[32,2,32,4,192]{4,3,2,1,0:T(4,128)(2,1)} %reshape_reshape.3), kind=kOutput, calls=%fused_computation.8 | convolution fusion | flops 6442450944 | bytes 24117248 | tf_op jit(solution)/shard_map/secxf,secd->xefd/dot_general | solution.py:375
  185.8 8.2 %copy.68 = bf16[2,2048,4,192]{1,3,0,2:T(8,128)(2,1)} copy(f32[2,2048,4,192]{1,3,2,0:T(8,128)} %fusion.6) | data formatting | bytes 18874368 | tf_op jit(solution)/shard_map/secxf,secd->xefd/dot_general | solution.py:375
  194.0 2.1 constant_dynamic-slice_fusion
  196.1 82.0 %giveback.1 = (bf16[32,64,768]{2,1,0:T(8,128)(2,1)}, bf16[3,2,192,2048]{3,2,1,0:T(8,128)(2,1)}) custom-call(bf16[32,64,768]{2,1,0:T(8,128)(2,1)} %reshape.67.back_ref, bf16[4,2,192,2048]{3,2,1,0:T(8,128)(2,1)} %bitcast.51), custom_call_target="tpu_custom_call" | custom-call | tf_op jit(solution)/shard_map/giveback/pallas_call | solution.py:234
  278.1 5.2 %convert_reduce_fusion = f32[2,192,2048]{2,1,0:T(8,128)} fusion(bf16[3,2,192,2048]{3,2,1,0:T(8,128)(2,1)} %get-tuple-element.26), kind=kLoop, calls=%fused_computation.1 | loop fusion | flops 3932160 | bytes 7864320 | tf_op jit(solution)/shard_map/reduce_sum | solution.py:387
  283.3 4.0 %add.35 = f32[2,2,96,2048]{3,2,1,0:T(8,128)} add(f32[2,2,96,2048]{3,2,1,0:T(8,128)S(1)} %bitcast.54, f32[2,2,96,2048]{3,2,1,0:T(8,128)} %bitcast.55) | non-fusion elementwise | flops 786432 | bytes 9437184 | tf_op jit(solution)/shard_map/add | solution.py:387
  287.3 2.4 fusion.16
  289.7 5.5 %collective-permute-start = (bf16[2,96,2048]{2,1,0:T(8,128)(2,1)}, bf16[2,96,2048]{2,1,0:T(8,128)(2,1)}, u32[]{:S(2)}, u32[]{:S(2)}) collective-permute-start(bf16[2,96,2048]{2,1,0:T(8,128)(2,1)} %fusion.16), channel_id=1, source_target_pairs={{0,1},{1,0},{2,3},{3,2},{4,5},{5,4},{6,7},{7,6},{8,9},{9,8},{10,11... | collective-permute-start | bytes 2359304 | tf_op jit(solution)/shard_map/ppermute | solution.py:391
  296.3 1.0 copy.36.slot_ref
  297.3 7.7 %combine.1 = (bf16[1024,768]{1,0:T(8,128)(2,1)}, f32[1024,1]{1,0:T(8,128)}) custom-call(s32[1024,1]{1,0:T(8,128)} %copy.36.slot_ref, f32[1024,1]{1,0:T(8,128)} %reshape.75.gate_ref, bf16[1024,768]{1,0:T(8,128)(2,1)} %bitcast.56, bf16[2048,768]{1,0:T(8,128)(2,1)} %bitcast.58), custom_call_target="tpu_custom_call" | custom-call | tf_op jit(solution)/shard_map/combine/pallas_call | solution.py:315
  305.0 1.2 reduce
  307.0 23.0 %collective-permute-done = bf16[2,96,2048]{2,1,0:T(8,128)(2,1)} collective-permute-done((bf16[2,96,2048]{2,1,0:T(8,128)(2,1)}, bf16[2,96,2048]{2,1,0:T(8,128)(2,1)}, u32[]{:S(2)}, u32[]{:S(2)}) %collective-permute-start) | collective-permute-done | bytes 786464 | tf_op jit(solution)/shard_map/ppermute | solution.py:391
  330.0 5.6 %fusion.18 = (bf16[2,96,2048]{2,1,0:T(8,128)(2,1)}, f32[2,96,2048]{2,1,0:T(8,128)}, bf16[2,96,2048]{2,1,0:T(8,128)(2,1)}) fusion(bf16[2,96,2048]{2,1,0:T(8,128)(2,1)} %collective-permute-done, f32[2,2,96,2048]{3,2,1,0:T(8,128)S(1)} %copy-done, s32[]{:T(128)S(6)} %select_n.12, bf16[2,96,2048]{2,1,0:T(8,128)(2,1)} %param.17, f32[2,96,2048]{2,1,0:T(8,128)} %param.15, ...), kind=kLoop, calls=%fused_computation.24 | loop fusion | flops 8257536 | bytes 8650756 | tf_op jit(solution)/shard_map/convert_element_type | solution.py:402
  (19 shorter events, 6.0 us)
Async XLA Ops:
  8.9 3.0 copy-start.2
  159.6 8.4 %copy-start.1 = (bf16[32,64,768]{2,1,0:T(8,128)(2,1)S(1)}, bf16[32,64,768]{2,1,0:T(8,128)(2,1)}, u32[]{:S(2)}) copy-start(bf16[32,64,768]{2,1,0:T(8,128)(2,1)} %get-tuple-element.22) | copy-start | bytes 9437188
  283.3 13.0 %copy-start.3 = (s32[1,1024]{1,0:T(1,128)S(1)}, s32[1,1024]{1,0:T(1,128)}, u32[]{:S(2)}) copy-start(s32[1,1024]{1,0:T(1,128)} %get-tuple-element.16) | copy-start | bytes 12292
  289.7 40.2 %collective-permute-start = (bf16[2,96,2048]{2,1,0:T(8,128)(2,1)}, bf16[2,96,2048]{2,1,0:T(8,128)(2,1)}, u32[]{:S(2)}, u32[]{:S(2)}) collective-permute-start(bf16[2,96,2048]{2,1,0:T(8,128)(2,1)} %fusion.16), channel_id=1, source_target_pairs={{0,1},{1,0},{2,3},{3,2},{4,5},{5,4},{6,7},{7,6},{8,9},{9,8},{10,11... | collective-permute-start | bytes 2359304 | tf_op jit(solution)/shard_map/ppermute | solution.py:391
  297.3 32.7 %copy-start = (f32[2,2,96,2048]{3,2,1,0:T(8,128)S(1)}, f32[2,2,96,2048]{3,2,1,0:T(8,128)}, u32[]{:S(2)}) copy-start(f32[2,2,96,2048]{3,2,1,0:T(8,128)} %add.35) | copy-start | bytes 9437188

commit v2 on v0

v2 whole, which is shorter than its diff:
```python
import jax
import jax.numpy as jnp
from jax import lax
from jax.experimental import pallas as pl
from jax.experimental.pallas import tpu as pltpu
from jax.sharding import PartitionSpec as P

MESH = pl.DeviceIdType.MESH
NY, NZ, NZL, NX = 4, 8, 4, 4
CAP = 32
F32, BF = jnp.float32, jnp.bfloat16
ANY = pl.BlockSpec(memory_space=pl.ANY)
VMEM = pl.BlockSpec(memory_space=pltpu.VMEM)


class Place:
    def __init__(self):
        self.own = lax.axis_index("expert")
        self.core = lax.rem(self.own, 2)
        self.y = self.own // (2 * NZL)
        self.half = lax.axis_index("replica")
        self.z = self.half * NZL + lax.rem(self.own // 2, NZL)
        self.x = lax.axis_index("fsdp")
        self.s = 1 - 2 * self.core

    def slot(self, dy, dz, core):
        y = lax.rem(self.y + dy + NY, NY)
        zl = lax.rem(self.z + dz + NZ, NZL)
        return (y * NZL + zl) * 2 + core

    def dev(self, dy, dz, core):
        return {
            "expert": self.slot(dy, dz, core),
            "replica": lax.rem(self.z + dz + NZ, NZ) // NZL,
        }

    def dev_x(self, dx):
        return {"fsdp": lax.rem(self.x + dx + NX, NX)}

    def around(self, i):
        return self.s * ((1 - i % 2) * (i // 2) - (i % 2) * ((i + 1) // 2))


def remote(src, dst, ssem, rsem, dev):
    return pltpu.make_async_remote_copy(
        src_ref=src, dst_ref=dst, send_sem=ssem, recv_sem=rsem, device_id=dev, device_id_type=MESH
    )


def peers(p, far):
    out = []
    for dy in (2, 1, -1, 0):
        for kind in (2, 1, 3, 0):
            for dc in (0, 1):
                core = p.core if dc == 0 else 1 - p.core
                if dc == 0 and dy == 0 and kind == 0:
                    continue
                dz = (0, 1, far(core), -1)[kind]
                out.append((p.dev(dy, dz, core), dy))
    return out


def before(n):
    row = lax.broadcasted_iota(jnp.int32, (n, n), 0)
    return (row < lax.broadcasted_iota(jnp.int32, (n, n), 1)).astype(F32).astype(BF)


def whole_kernel(
    dy_ref, ids_ref, ids_t_ref, hid_ref, gate_ref, ids_c_ref, wq_ref, we_ref,
    hg_ref, gg_ref, gs_ref,
    rdy, rids, rw, ws, wf, xs, wt, own_g, rg, rback, ez_s, ez_r, code, g_tile,
    dy_ss, dy_rs, sib_ss, sib_rs, id_ss, id_rs, b_ss, b_rs, w_ss, w_rs, d_ss, d_rs, e_ss, e_rs,
    z_ss, z_rs, l_sem,
):
    p = Place()
    core, s = p.core, p.s
    tokens, width = dy_ref.shape
    held, rows, _ = wq_ref.shape
    routes, hid = hid_ref.shape
    groups = rids.shape[0]
    half = tokens // 2
    slots = held * CAP
    early, dys = [], []
    count = [0, 0, 0]

    def start(c, to):
        c.start()
        to.append(c)

    def part(slot, h):
        return rdy.at[pl.ds(pl.multiple_of(slot * tokens + h * half, half), half)]

    def block(slot):
        return rdy.at[pl.ds(pl.multiple_of(slot * tokens, tokens), tokens)]

    def at(h, a, b):
        return (a, b) if h == 0 else (b, a)

    def send_dy(src, slot, h, dev):
        k = count[h]
        count[h] += 1
        start(remote(src, part(slot, h), dy_ss.at[h, k], dy_rs.at[h, slot], dev), dys)

    def wait_dy(slot, h):
        blk = part(slot, h)
        remote(blk, blk, dy_ss.at[h, 0], dy_rs.at[h, slot], p.dev(1, 0, core)).wait_recv()

    def send_sib(src, slot):
        k = count[2]
        count[2] += 1
        start(remote(src, block(slot), sib_ss.at[k], sib_rs.at[slot], p.dev(0, 0, 1 - core)), dys)

    def wait_sib(slot):
        blk = block(slot)
        remote(blk, blk, sib_ss.at[0], sib_rs.at[slot], p.dev(0, 0, 1 - core)).wait_recv()

    def mine(h):
        return dy_ref.at[pl.ds(h * half, half)]

    for h in (0, 1):
        for d in (1, -1):
            send_dy(mine(h), p.own, h, p.dev(*at(h, d, 0), core))
    for h in (0, 1):
        for d in (1, -1):
            send_dy(mine(h), p.own, h, p.dev(*at(h, 0, d), core))
    send_sib(dy_ref, p.own)
    there = peers(p, lambda c: 2 * s)
    for k, (dev, _) in enumerate(there):
        start(remote(ids_t_ref, rids.at[p.own], id_ss.at[k], id_rs.at[p.own], dev), early)
    local = [
        pltpu.make_async_copy(dy_ref, block(p.own), l_sem.at[0]),
        pltpu.make_async_copy(ids_t_ref, rids.at[p.own], l_sem.at[1]),
    ]
    for c in local:
        c.start()

    def shard(x):
        return wf.at[:, pl.ds(pl.multiple_of(x * rows, rows), rows)]

    mine_w = pl.ds(pl.multiple_of(p.x * rows, rows), rows)
    qb = width // we_ref.shape[2]
    for e in range(held):
        scale = jnp.exp2(we_ref[e].astype(F32))
        for j in range(we_ref.shape[2]):
            cols = pl.ds(j * qb, qb)
            wf[e, mine_w, cols] = (wq_ref[e, :, cols].astype(F32) * scale[:, j : j + 1]).astype(BF)

    experts = groups * held
    ids = ids_ref[...]
    named = jnp.where(
        ids == lax.broadcasted_iota(jnp.int32, (experts, routes), 0), 1.0, 0.0
    ).astype(F32)
    rank = jnp.dot(named.astype(BF), before(routes), preferred_element_type=F32)
    slot_row = ids * CAP + jnp.sum(named * rank, axis=0, keepdims=True).astype(jnp.int32)
    hg_ref[...] = (gate_ref[...] * hid_ref[...].astype(F32)).astype(BF)

    for i, dx in enumerate((1, -1)):
        start(remote(shard(p.x), shard(p.x), w_ss.at[i], w_rs.at[p.x], p.dev_x(dx)), early)

    step = 256
    per = step // slots

    def fill(i, _):
        lo = i * step
        pick = (slot_row == lax.broadcasted_iota(jnp.int32, (step, routes), 0) + lo).astype(F32)
        got = jnp.dot(pick.astype(BF), hg_ref[...], preferred_element_type=F32).astype(BF)
        ws[pl.ds(i * per, per)] = got.reshape(per, slots, hid)
        return 0

    lax.fori_loop(0, groups // per, fill, 0)

    for h in (0, 1):
        b = p.slot(*at(h, -s, 0), core)
        wait_dy(b, h)
        send_dy(part(b, h), b, h, p.dev(*at(h, s, 0), core))
        for d in (1, -1):
            send_dy(part(b, h), b, h, p.dev(*at(h, 0, d), core))

    def send_rows(lo, hi):
        for k in range(lo, hi):
            dev = there[k][0]
            start(remote(ws.at[dev["expert"]], rw.at[p.own], b_ss.at[k], b_rs.at[p.own], dev), early)

    own_rows = pltpu.make_async_copy(ws.at[p.own], rw.at[p.own], l_sem.at[2])
    own_rows.start()
    send_rows(0, 8)
    for a in (s, -2 * s):
        for h in (0, 1):
            b = p.slot(*at(h, a, 0), core)
            wait_dy(b, h)
            for d in (1, -1):
                send_dy(part(b, h), b, h, p.dev(*at(h, 0, d), core))
    send_rows(8, 16)
    for a in (0, -s, s, -2 * s):
        for h in (0, 1):
            b = p.slot(*at(h, a, -s), core)
            wait_dy(b, h)
            send_dy(part(b, h), b, h, p.dev(*at(h, 0, s), core))
    send_rows(16, 31)

    back_x = lax.rem(p.x - s + NX, NX)
    remote(shard(back_x), shard(back_x), w_ss.at[2], w_rs.at[back_x], p.dev_x(s)).wait_recv()
    start(remote(shard(back_x), shard(back_x), w_ss.at[2], w_rs.at[back_x], p.dev_x(s)), early)

    local[1].wait()
    for dc in (0, 1):
        c2 = core if dc == 0 else 1 - core
        for dy in range(NY):
            for dz in range(NZL):
                if dc == 0 and dy == 0 and dz == 0:
                    continue
                j = p.slot(dy, dz, c2)
                remote(
                    rids.at[j], rids.at[j], id_ss.at[0], id_rs.at[j], p.dev(1, 0, core)
                ).wait_recv()
    tri = before(tokens)
    for e in range(held):
        hit = jnp.sum((rids[...] == p.own * held + e).astype(F32), axis=1)
        code[e] = jnp.where(
            hit > 0, jnp.dot(hit.astype(BF), tri, preferred_element_type=F32), -1.0
        )

    def pick_rows(j):
        lane = lax.broadcasted_iota(jnp.int32, (CAP, tokens), 0).astype(F32)
        pick = jnp.concatenate(
            [(code[e, pl.ds(j, 1), :] == lane).astype(F32) for e in range(held)], axis=0
        ).astype(BF)
        got = jnp.dot(pick, block(j)[...], preferred_element_type=F32).astype(BF)
        for e in range(held):
            xs[e, pl.ds(pl.multiple_of(j * CAP, CAP), CAP)] = got[e * CAP : (e + 1) * CAP]

    def pair(g, k):
        t = g // (k + 1)
        return (1 - t) * g + t * k, (1 - t) * k + t * (g - k - 1)

    def own_stage(k):
        offs = (0, -s, s, -2 * s)
        pairs = [(i, k) for i in range(k)] + [(k, j) for j in range(k)] + [(k, k)]
        for i, j in pairs:
            b = p.slot(offs[i], offs[j], core)
            if j > 1:
                wait_dy(b, 0)
            if i > 1:
                wait_dy(b, 1)
            send_sib(block(b), b)

        def one(g, _):
            i, j = pair(g, k)
            pick_rows(p.slot(p.around(i), p.around(j), core))
            return 0

        lax.fori_loop(0, 2 * k + 1, one, 0)

    def sib_stage(k):
        def one(g, _):
            i, j = pair(g, k)
            b = p.slot(-p.around(i), -p.around(j), 1 - core)
            wait_sib(b)
            pick_rows(b)
            return 0

        lax.fori_loop(0, 2 * k + 1, one, 0)

    local[0].wait()
    pick_rows(p.own)
    own_stage(1)
    sib_stage(0)
    own_stage(2)
    sib_stage(1)
    own_stage(3)
    sib_stage(2)
    sib_stage(3)

    own_rows.wait()
    for dc in (0, 1):
        c2 = core if dc == 0 else 1 - core
        for dy in range(NY):
            for dz in range(NZL):
                if dc == 0 and dy == 0 and dz == 0:
                    continue
                j = p.slot(dy, dz, c2)
                remote(rw.at[j], rw.at[j], b_ss.at[0], b_rs.at[j], p.dev(1, 0, core)).wait_recv()
    for c in dys:
        c.wait_send()

    chunk = groups * CAP // 4
    for e in range(held):
        for i in range(4):
            got = rw[i * 8 : (i + 1) * 8, e * CAP : (e + 1) * CAP].reshape(chunk, hid)
            wt[e, :, i * chunk : (i + 1) * chunk] = got.T
    piece = width // 2
    nt = 256
    own_at = pl.ds(pl.multiple_of(p.x * rows, rows), rows)
    late = []
    for e in range(held):
        for h in (0, 1):

            def tile(n, _):
                cols = pl.ds(pl.multiple_of(h * piece + n * nt, nt), nt)
                g = jnp.dot(wt[e], xs[e, :, cols], preferred_element_type=F32)
                rdy[e * hid : (e + 1) * hid, cols] = g.astype(BF)
                g_tile[...] = g
                own_g[e, :, cols] = g_tile[own_at]
                return 0

            lax.fori_loop(0, piece // nt, tile, 0)
            cols = pl.ds(h * piece, piece)
            for k, dx in enumerate((1, -1, 2)):
                to = lax.rem(p.x + dx + NX, NX)
                src = rdy.at[pl.ds(pl.multiple_of(e * hid + to * rows, rows), rows), cols]
                start(
                    remote(
                        src, rg.at[k, e, :, cols], e_ss.at[e, h, k], e_rs.at[e, h, k], p.dev_x(dx)
                    ),
                    late,
                )

    for dx in (1, 2):
        j = lax.rem(p.x + dx * s + 2 * NX, NX)
        remote(shard(j), shard(j), w_ss.at[0], w_rs.at[j], p.dev_x(1)).wait_recv()
    for c in early:
        c.wait_send()
    home = peers(p, lambda c: 4 * c - 2)
    k = 0
    for dy in (2, 1, -1, 0):
        yy = lax.rem(p.y + dy + NY, NY)
        for e in range(held):
            x_rows = xs[e, pl.ds(pl.multiple_of(yy * 256, 256), 256)]
            got = lax.dot_general(
                x_rows, wf[e], (((1,), (1,)), ((), ())), preferred_element_type=F32
            )
            ws[pl.ds(yy * 8, 8), e * CAP : (e + 1) * CAP] = got.astype(BF).reshape(8, CAP, hid)
        for dev, dy2 in home:
            if dy2 == dy:
                start(
                    remote(
                        ws.at[dev["expert"]], rback.at[p.own], d_ss.at[k], d_rs.at[p.own], dev
                    ),
                    late,
                )
                k += 1
    own_back = pltpu.make_async_copy(ws.at[p.own], rback.at[p.own], l_sem.at[3])
    own_back.start()

    keep = rows // 2

    def reduce_piece(e, h):
        cols = pl.ds(h * piece, piece)
        for k in range(3):
            a = rg.at[k, e, :, cols]
            remote(a, a, e_ss.at[e, h, k], e_rs.at[e, h, k], p.dev_x(1)).wait_recv()

        def total(r):
            at_r = pl.ds(pl.multiple_of(r * keep, keep), keep)
            t = own_g[e, at_r, cols]
            for k in range(3):
                t += rg[k, e, at_r, cols].astype(F32)
            return t

        ez_s[e, :, cols] = total(1 - p.half).astype(BF)
        gs_ref[e, :, cols] = total(p.half)
        start(
            remote(
                ez_s.at[e, :, cols], ez_r.at[e, :, cols], z_ss.at[e, h], z_rs.at[e, h],
                {"replica": 1 - p.half},
            ),
            late,
        )

    reduce_piece(0, 0)
    reduce_piece(0, 1)

    own_back.wait()
    for dc in (0, 1):
        c2 = core if dc == 0 else 1 - core
        for dy in range(NY):
            for dz in range(NZL):
                if dc == 0 and dy == 0 and dz == 0:
                    continue
                j = p.slot(dy, dz, c2)
                remote(
                    rback.at[j], rback.at[j], d_ss.at[0], d_rs.at[j], p.dev(1, 0, core)
                ).wait_recv()

    named_c = ids_c_ref[...] == lax.broadcasted_iota(jnp.int32, (routes, experts), 1)
    named_c = jnp.where(named_c, 1.0, 0.0).astype(BF)

    def join(i, _):
        r = pl.ds(pl.multiple_of(i * step, step), step)
        here = lax.broadcasted_iota(jnp.int32, (step, routes), 0) + i * step
        older = (lax.broadcasted_iota(jnp.int32, (step, routes), 1) < here).astype(F32)
        rank = jnp.dot(older.astype(BF), named_c, preferred_element_type=F32)
        mine = ids_c_ref[r] == lax.broadcasted_iota(jnp.int32, (step, experts), 1)
        rank = jnp.sum(jnp.where(mine, rank, 0.0), axis=1, keepdims=True)
        slot_c = ids_c_ref[r] * CAP + rank.astype(jnp.int32)
        pick = slot_c == lax.broadcasted_iota(jnp.int32, (step, groups * slots), 1)
        got = jnp.dot(
            pick.astype(F32).astype(BF),
            rback[...].reshape(groups * slots, hid),
            preferred_element_type=F32,
        )
        hg_ref[r] = (gate_ref[r] * got).astype(BF)
        gg_ref[r] = jnp.sum(hid_ref[r].astype(F32) * got, axis=1, keepdims=True)
        return 0

    lax.fori_loop(0, routes // step, join, 0)

    reduce_piece(1, 0)
    reduce_piece(1, 1)
    for e in range(held):
        for h in (0, 1):
            cols = pl.ds(h * piece, piece)
            a = ez_r.at[e, :, cols]
            remote(a, a, z_ss.at[e, h], z_rs.at[e, h], p.dev_x(1)).wait_recv()
            gs_ref[e, :, cols] += ez_r[e, :, cols].astype(F32)
    for c in late:
        c.wait_send()


def whole(dy, ids, ids_t, hidden, gate, ids_c, wq, we):
    tokens, width = dy.shape
    held, rows, _ = wq.shape
    routes, hid = hidden.shape
    groups = lax.axis_size("expert")
    slots = held * CAP
    full = rows * NX
    dma = pltpu.SemaphoreType.DMA
    vm = pltpu.VMEM
    return pl.pallas_call(
        whole_kernel,
        out_shape=(
            jax.ShapeDtypeStruct((routes, hid), BF),
            jax.ShapeDtypeStruct((routes, 1), F32),
            jax.ShapeDtypeStruct((held, rows // 2, width), F32),
        ),
        in_specs=[VMEM] * 8,
        out_specs=(VMEM,) * 3,
        scratch_shapes=[
            vm((groups * tokens, width), BF),
            vm((groups,) + ids_t.shape, jnp.int32),
            vm((groups, slots, hid), BF),
            vm((groups, slots, hid), BF),
            vm((held, full, width), BF),
            vm((held, groups * CAP, width), BF),
            vm((held, hid, groups * CAP), BF),
            vm((held, rows, width), F32),
            vm((NX - 1, held, rows, width), BF),
            vm((groups, slots, hid), BF),
            vm((held, rows // 2, width), BF),
            vm((held, rows // 2, width), BF),
            vm((held, groups, tokens), F32),
            vm((hid, 256), F32),
            dma((2, 15)), dma((2, 32)), dma((16,)), dma((32,)), dma((31,)), dma((32,)),
            dma((31,)), dma((32,)), dma((3,)), dma((4,)), dma((31,)), dma((32,)),
            dma((2, 2, 3)), dma((2, 2, 3)), dma((2, 2)), dma((2, 2)), dma((4,)),
        ],
        compiler_params=pltpu.CompilerParams(
            has_side_effects=True, vmem_limit_bytes=67043328
        ),
        name="whole",
    )(dy, ids, ids_t, hidden, gate, ids_c, wq, we)


def body(
    out_grad, hidden_saved, gate_probs, expert_ids, weight_q, weight_exp, master, moment1, moment2
):
    tokens, top = expert_ids.shape
    hid = hidden_saved.shape[2]
    routes = tokens * top

    ids = expert_ids.reshape(1, routes)
    hidden_grad, gate_grad, gradient = whole(
        out_grad,
        ids,
        expert_ids.T,
        hidden_saved.reshape(routes, hid),
        gate_probs.reshape(routes, 1),
        expert_ids.reshape(routes, 1),
        weight_q,
        weight_exp,
    )
    first = 0.9 * moment1.astype(F32) + 0.1 * gradient
    second = 0.95 * moment2.astype(F32) + 0.05 * gradient * gradient
    update = first / (1.0 - 0.9**20) / (jnp.sqrt(second / (1.0 - 0.95**20)) + 1e-08) + 0.1 * master
    return (
        hidden_grad.reshape(tokens, top, hid),
        gate_grad.reshape(tokens, top),
        master - 0.001 * update,
        first.astype(BF),
        second.astype(BF),
    )


def solution(mesh):
    tok = ("expert", "fsdp", "replica")
    in_specs = (
        P(tok, None),
        P(tok, None, None),
        P(tok, None),
        P(tok, None),
        P("expert", "fsdp", None),
        P("expert", "fsdp", None),
        P("expert", ("fsdp", "replica"), None),
        P("expert", ("fsdp", "replica"), None),
        P("expert", ("fsdp", "replica"), None),
    )
    out_specs = (
        P(tok, None, None),
        P(tok, None),
        P("expert", ("fsdp", "replica"), None),
        P("expert", ("fsdp", "replica"), None),
        P("expert", ("fsdp", "replica"), None),
    )
    return jax.shard_map(body, mesh=mesh, in_specs=in_specs, out_specs=out_specs, check_vma=False)
```

time: 565 us -> 233 us (0.41)
  the two profiles are of different devices: /device:TPU:32 before, /device:TPU:65 now
where the time goes in v2:
time: 233 us
  Pallas kernels  217 us (93%)
  local copies, waits for them, and re-layouts  7.67 us (3%)
  other arithmetic  7.17 us (3%)
    pallas_call x1, Pallas kernels, whole(): pl.pallas_call(whole_kernel, out_shape=(jax.ShapeDtypeStruct((routes, hid...  217 us
    convert_element_type x1, other arithmetic, body(): second.astype(BF)  5.92 us
    unnamed x7, local copies, waits for them, and re-layouts  4.93 us

profile of v2, /device:TPU:65, one launch (start us, length us, event | category | flops | bytes accessed | tf_op | source)
XLA Modules:
  0.0 232.8 jit_solution(10347166759021548570)
XLA Ops:
  0.6 0.8 copy.19
  1.4 0.7 reshape.28.ids_ref
  2.1 0.8 copy.20
  2.9 1.6 copy.24.we_ref
  4.4 1.0 reshape.34.gate_ref
  5.4 1.0 reshape.35.ids_c_ref
  6.4 217.3 %whole.1 = (bf16[1024,768]{1,0:T(8,128)(2,1)}, f32[1024,1]{1,0:T(8,128)}, f32[2,96,2048]{2,1,0:T(8,128)}) custom-call(bf16[128,2048]{1,0:T(8,128)(2,1)} %dy_ref.1, s32[1,1024]{1,0:T(1,128)} %reshape.28.ids_ref, s32[8,128]{1,0:T(8,128)} %bitcast.5, bf16[1024,768]{1,0:T(8,128)(2,1)} %bitcast.4, f32[1024,1]{1,0:T(8,128)} %reshape.34.gate_ref, ...), custom_call_target="tpu_custom_call" | custom-call | tf_op jit(solution)/shard_map/whole/pallas_call | solution.py:429
  223.7 1.2 reduce
  224.9 0.1 reshape.33
  225.0 0.7 copy.25
  225.7 0.0 copy-start
  225.7 5.9 %fusion.2 = (bf16[2,96,2048]{2,1,0:T(8,128)(2,1)}, f32[2,96,2048]{2,1,0:T(8,128)}, bf16[2,96,2048]{2,1,0:T(8,128)(2,1)}) fusion(f32[2,96,2048]{2,1,0:T(8,128)} %get-tuple-element.10, bf16[2,96,2048]{2,1,0:T(8,128)(2,1)} %param.17, f32[2,96,2048]{2,1,0:T(8,128)} %param.15, bf16[2,96,2048]{2,1,0:T(8,128)(2,1)} %param.16), kind=kLoop, calls=%fused_computation.5 | loop fusion | flops 7471104 | bytes 7864320 | tf_op jit(solution)/shard_map/convert_element_type | solution.py:490
  231.6 0.0 copy-done
  231.6 1.1 copy.27
Async XLA Ops:
  225.7 5.9 %copy-start = (bf16[1024,768]{1,0:T(8,128)(2,1)S(1)}, bf16[1024,768]{1,0:T(8,128)(2,1)}, u32[]{:S(2)}) copy-start(bf16[1024,768]{1,0:T(8,128)(2,1)} %get-tuple-element.8) | copy-start | bytes 4718596

commit v3 on v2

--- a/solution.py
+++ b/solution.py
@@ -49,7 +49,7 @@
 
 def peers(p, far):
     out = []
-    for dy in (2, 1, -1, 0):
+    for dy in (1, -1, 0):
         for kind in (2, 1, 3, 0):
             for dc in (0, 1):
                 core = p.core if dc == 0 else 1 - p.core
@@ -60,17 +60,33 @@
     return out
 
 
+def far_row(p, dy, far):
+    return [
+        p.dev(dy, (0, 1, far(c), -1)[kind], c)
+        for kind in range(NZL)
+        for c in (p.core, 1 - p.core)
+    ]
+
+
+def spread(rows):
+    k, t = rows.shape
+    wide = jnp.broadcast_to(rows[None], (t, k, t)).reshape(t * k, t)
+    at_t = lax.broadcasted_iota(jnp.int32, (t * k, t), 0) // k
+    here = at_t == lax.broadcasted_iota(jnp.int32, (t * k, t), 1)
+    return jnp.sum(jnp.where(here, wide, jnp.zeros_like(wide)), axis=1, keepdims=True)
+
+
 def before(n):
     row = lax.broadcasted_iota(jnp.int32, (n, n), 0)
     return (row < lax.broadcasted_iota(jnp.int32, (n, n), 1)).astype(F32).astype(BF)
 
 
 def whole_kernel(
-    dy_ref, ids_ref, ids_t_ref, hid_ref, gate_ref, ids_c_ref, wq_ref, we_ref,
+    dy_ref, ids_t_ref, hid_ref, gate_ref, wq_ref, we_ref,
     hg_ref, gg_ref, gs_ref,
-    rdy, rids, rw, ws, wf, xs, wt, own_g, rg, rback, ez_s, ez_r, code, g_tile,
+    rdy, rids, rw, ws, wf, xs, wt, own_g, rg, rback, b_via, d_via, ez_s, ez_t, ez_r, code, g_tile,
     dy_ss, dy_rs, sib_ss, sib_rs, id_ss, id_rs, b_ss, b_rs, w_ss, w_rs, d_ss, d_rs, e_ss, e_rs,
-    z_ss, z_rs, l_sem,
+    v_rs, z_ss, z_rs, l_sem,
 ):
     p = Place()
     core, s = p.core, p.s
@@ -114,6 +130,14 @@
         blk = block(slot)
         remote(blk, blk, sib_ss.at[0], sib_rs.at[slot], p.dev(0, 0, 1 - core)).wait_recv()
 
+    gate = pltpu.get_barrier_semaphore()
+    near = [dev for dev, _ in peers(p, lambda c: 2 * s)] + far_row(p, 2, lambda c: 2 * s)
+    near += [p.dev(dy, -2 * s, core) for dy in range(NY)]
+    near += [p.dev_x(d) for d in (1, 2, 3)] + [{"replica": 1 - p.half}]
+    for dev in near:
+        pl.semaphore_signal(gate, inc=1, device_id=dev, device_id_type=MESH)
+    pl.semaphore_wait(gate, len(near))
+
     def mine(h):
         return dy_ref.at[pl.ds(h * half, half)]
 
@@ -125,7 +149,7 @@
             send_dy(mine(h), p.own, h, p.dev(*at(h, 0, d), core))
     send_sib(dy_ref, p.own)
     there = peers(p, lambda c: 2 * s)
-    for k, (dev, _) in enumerate(there):
+    for k, dev in enumerate([dev for dev, _ in there] + far_row(p, 2, lambda c: 2 * s)):
         start(remote(ids_t_ref, rids.at[p.own], id_ss.at[k], id_rs.at[p.own], dev), early)
     local = [
         pltpu.make_async_copy(dy_ref, block(p.own), l_sem.at[0]),
@@ -138,21 +162,48 @@
         return wf.at[:, pl.ds(pl.multiple_of(x * rows, rows), rows)]
 
     mine_w = pl.ds(pl.multiple_of(p.x * rows, rows), rows)
-    qb = width // we_ref.shape[2]
+    qb = width // we_ref.shape[1]
     for e in range(held):
-        scale = jnp.exp2(we_ref[e].astype(F32))
-        for j in range(we_ref.shape[2]):
+        blocks = we_ref.shape[1]
+        same = lax.broadcasted_iota(jnp.int32, (blocks, blocks), 0) == lax.broadcasted_iota(
+            jnp.int32, (blocks, blocks), 1
+        )
+        power = lax.dot_general(
+            we_ref[e].astype(F32).astype(BF), same.astype(F32).astype(BF),
+            (((0,), (0,)), ((), ())), preferred_element_type=F32,
+        )
+        scale = jnp.exp2(power)
+        for j in range(blocks):
             cols = pl.ds(j * qb, qb)
             wf[e, mine_w, cols] = (wq_ref[e, :, cols].astype(F32) * scale[:, j : j + 1]).astype(BF)
 
     experts = groups * held
-    ids = ids_ref[...]
-    named = jnp.where(
-        ids == lax.broadcasted_iota(jnp.int32, (experts, routes), 0), 1.0, 0.0
-    ).astype(F32)
-    rank = jnp.dot(named.astype(BF), before(routes), preferred_element_type=F32)
-    slot_row = ids * CAP + jnp.sum(named * rank, axis=0, keepdims=True).astype(jnp.int32)
-    hg_ref[...] = (gate_ref[...] * hid_ref[...].astype(F32)).astype(BF)
+    ids_t = ids_t_ref[...]
+    top = ids_t.shape[0]
+    expert = lax.broadcasted_iota(jnp.int32, (experts, tokens), 0)
+    named = jnp.zeros((experts, tokens), F32)
+    for k in range(top):
+        named += (ids_t[k : k + 1] == expert).astype(F32)
+    rank = jnp.dot(named.astype(BF), before(tokens), preferred_element_type=F32)
+    rank_t = jnp.concatenate(
+        [
+            jnp.sum(jnp.where(ids_t[k : k + 1] == expert, rank, 0.0), axis=0, keepdims=True)
+            for k in range(top)
+        ],
+        axis=0,
+    )
+    slot_t = ids_t * CAP + rank_t.astype(jnp.int32)
+    both = jnp.concatenate([ids_t.astype(F32), rank_t], axis=0).astype(BF)
+    lane_t = lax.broadcasted_iota(jnp.int32, (tokens, routes), 1) // top
+    over = (lane_t == lax.broadcasted_iota(jnp.int32, (tokens, routes), 0)).astype(F32)
+    both = jnp.dot(both, over.astype(BF), preferred_element_type=F32)
+    mine_k = lax.rem(
+        lax.broadcasted_iota(jnp.int32, (top, routes), 1), top
+    ) == lax.broadcasted_iota(jnp.int32, (top, routes), 0)
+    slot_row = jnp.sum(
+        jnp.where(mine_k, both[:top] * CAP + both[top:], 0.0), axis=0, keepdims=True
+    ).astype(jnp.int32)
+    hg_ref[...] = (spread(gate_ref[...]) * hid_ref[...].astype(F32)).astype(BF)
 
     for i, dx in enumerate((1, -1)):
         start(remote(shard(p.x), shard(p.x), w_ss.at[i], w_rs.at[p.x], p.dev_x(dx)), early)
@@ -176,27 +227,51 @@
         for d in (1, -1):
             send_dy(part(b, h), b, h, p.dev(*at(h, 0, d), core))
 
-    def send_rows(lo, hi):
-        for k in range(lo, hi):
+    def of_expert(ref, j, e):
+        return ref.at[j, pl.ds(e * CAP, CAP)]
+
+    row_sends = [[] for _ in range(held)]
+
+    def far_rows(ref, e, y):
+        y = lax.rem(y + 2 * NY, NY)
+        return ref.at[pl.ds(y * 2 * NZL, 2 * NZL), pl.ds(e * CAP, CAP)]
+
+    def send_rows(e):
+        far = far_rows(ws, e, p.y + 2)
+        via = b_via.at[:, pl.ds(e * CAP, CAP)]
+        start(remote(far, via, b_ss.at[e, 31], v_rs.at[0, e], p.dev(s, 0, core)), row_sends[e])
+        for k in range(23):
             dev = there[k][0]
-            start(remote(ws.at[dev["expert"]], rw.at[p.own], b_ss.at[k], b_rs.at[p.own], dev), early)
+            src, dst = of_expert(ws, dev["expert"], e), of_expert(rw, p.own, e)
+            start(remote(src, dst, b_ss.at[e, k], b_rs.at[e, p.own], dev), row_sends[e])
+
+    def pass_rows(via, dst, e, k, ss, rs, far, to):
+        blk = via.at[:, pl.ds(e * CAP, CAP)]
+        remote(blk, blk, ss.at[e, 31], v_rs.at[k, e], p.dev(s, 0, core)).wait_recv()
+        origin = p.slot(-s, 0, core)
+        for i, dev in enumerate(far_row(p, s, far)):
+            src = of_expert(via, lax.rem(dev["expert"], 2 * NZL), e)
+            start(
+                remote(src, of_expert(dst, origin, e), ss.at[e, 23 + i], rs.at[e, origin], dev), to
+            )
 
     own_rows = pltpu.make_async_copy(ws.at[p.own], rw.at[p.own], l_sem.at[2])
     own_rows.start()
-    send_rows(0, 8)
+    send_rows(0)
     for a in (s, -2 * s):
         for h in (0, 1):
             b = p.slot(*at(h, a, 0), core)
             wait_dy(b, h)
             for d in (1, -1):
                 send_dy(part(b, h), b, h, p.dev(*at(h, 0, d), core))
-    send_rows(8, 16)
+    pass_rows(b_via, rw, 0, 0, b_ss, b_rs, lambda c: 2 * s, row_sends[0])
     for a in (0, -s, s, -2 * s):
         for h in (0, 1):
             b = p.slot(*at(h, a, -s), core)
             wait_dy(b, h)
             send_dy(part(b, h), b, h, p.dev(*at(h, 0, s), core))
-    send_rows(16, 31)
+    send_rows(1)
+    pass_rows(b_via, rw, 1, 0, b_ss, b_rs, lambda c: 2 * s, row_sends[1])
 
     back_x = lax.rem(p.x - s + NX, NX)
     remote(shard(back_x), shard(back_x), w_ss.at[2], w_rs.at[back_x], p.dev_x(s)).wait_recv()
@@ -271,153 +346,200 @@
     sib_stage(2)
     sib_stage(3)
 
-    own_rows.wait()
-    for dc in (0, 1):
-        c2 = core if dc == 0 else 1 - core
-        for dy in range(NY):
-            for dz in range(NZL):
-                if dc == 0 and dy == 0 and dz == 0:
-                    continue
-                j = p.slot(dy, dz, c2)
-                remote(rw.at[j], rw.at[j], b_ss.at[0], b_rs.at[j], p.dev(1, 0, core)).wait_recv()
     for c in dys:
         c.wait_send()
+    own_rows.wait()
+
+    def others():
+        for dc in (0, 1):
+            c2 = core if dc == 0 else 1 - core
+            for dy in range(NY):
+                for dz in range(NZL):
+                    if dc or dy or dz:
+                        yield p.slot(dy, dz, c2)
 
     chunk = groups * CAP // 4
-    for e in range(held):
+    piece = width // 2
+    nt = 256
+    late = []
+
+    def rows_of(e, x):
+        x = lax.rem(x + 2 * NX, NX)
+        return pl.ds(pl.multiple_of(e * hid + x * rows, rows), rows)
+
+    def weighted_here(e):
+        for j in others():
+            a = of_expert(rw, j, e)
+            remote(a, a, b_ss.at[e, 0], b_rs.at[e, j], p.dev(1, 0, core)).wait_recv()
+        for c in row_sends[e]:
+            c.wait_send()
         for i in range(4):
             got = rw[i * 8 : (i + 1) * 8, e * CAP : (e + 1) * CAP].reshape(chunk, hid)
             wt[e, :, i * chunk : (i + 1) * chunk] = got.T
-    piece = width // 2
-    nt = 256
-    own_at = pl.ds(pl.multiple_of(p.x * rows, rows), rows)
-    late = []
-    for e in range(held):
-        for h in (0, 1):
-
-            def tile(n, _):
-                cols = pl.ds(pl.multiple_of(h * piece + n * nt, nt), nt)
-                g = jnp.dot(wt[e], xs[e, :, cols], preferred_element_type=F32)
-                rdy[e * hid : (e + 1) * hid, cols] = g.astype(BF)
-                g_tile[...] = g
-                own_g[e, :, cols] = g_tile[own_at]
-                return 0
-
-            lax.fori_loop(0, piece // nt, tile, 0)
-            cols = pl.ds(h * piece, piece)
-            for k, dx in enumerate((1, -1, 2)):
-                to = lax.rem(p.x + dx + NX, NX)
-                src = rdy.at[pl.ds(pl.multiple_of(e * hid + to * rows, rows), rows), cols]
-                start(
-                    remote(
-                        src, rg.at[k, e, :, cols], e_ss.at[e, h, k], e_rs.at[e, h, k], p.dev_x(dx)
-                    ),
-                    late,
-                )
-
+
+    def to_x(e, h, k, x, dx):
+        cols = pl.ds(h * piece, piece)
+        src = rdy.at[rows_of(e, x), cols]
+        dst = rg.at[k, e, :, cols]
+        start(remote(src, dst, e_ss.at[e, h, k], e_rs.at[e, h, k], p.dev_x(dx)), late)
+
+    def from_x(e, h, k):
+        a = rg.at[k, e, :, pl.ds(h * piece, piece)]
+        remote(a, a, e_ss.at[e, h, k], e_rs.at[e, h, k], p.dev_x(1)).wait_recv()
+
+    def grad_piece(e, h):
+        def tile(n, _):
+            cols = pl.ds(pl.multiple_of(h * piece + n * nt, nt), nt)
+            g = jnp.dot(wt[e], xs[e, :, cols], preferred_element_type=F32)
+            rdy[e * hid : (e + 1) * hid, cols] = g.astype(BF)
+            g_tile[...] = g
+            own_g[e, :, cols] = g_tile[mine_w]
+            return 0
+
+        lax.fori_loop(0, piece // nt, tile, 0)
+        to_x(e, h, 0, p.x + 2 * s, s)
+        to_x(e, h, 1, p.x - s, -s)
+
+    def relay_piece(e, h):
+        cols = pl.ds(h * piece, piece)
+        from_x(e, h, 0)
+        r = rows_of(e, p.x + s)
+        rdy[r, cols] = (rdy[r, cols].astype(F32) + rg[0, e, :, cols].astype(F32)).astype(BF)
+        to_x(e, h, 2, p.x + s, s)
+
+    def back_tile(e, dy):
+        yy = lax.rem(p.y + dy + NY, NY)
+        x_rows = xs[e, pl.ds(pl.multiple_of(yy * 256, 256), 256)]
+        got = lax.dot_general(x_rows, wf[e], (((1,), (1,)), ((), ())), preferred_element_type=F32)
+        ws[pl.ds(yy * 8, 8), e * CAP : (e + 1) * CAP] = got.astype(BF).reshape(8, CAP, hid)
+
+    home = peers(p, lambda c: 4 * c - 2)
+
+    def back_rows(e):
+        for dy in (2, 1, -1, 0):
+            back_tile(e, dy)
+            if dy == 2:
+                far = far_rows(ws, e, p.y + 2)
+                via = d_via.at[:, pl.ds(e * CAP, CAP)]
+                c = remote(far, via, d_ss.at[e, 31], v_rs.at[1, e], p.dev(s, 0, core))
+                start(c, late)
+            for k, (dev, dy2) in enumerate(home):
+                if dy2 == dy:
+                    src, dst = of_expert(ws, dev["expert"], e), of_expert(rback, p.own, e)
+                    start(remote(src, dst, d_ss.at[e, k], d_rs.at[e, p.own], dev), late)
+
+    def pass_back(e):
+        pass_rows(d_via, rback, e, 1, d_ss, d_rs, lambda c: 4 * c - 2, late)
+
+    weighted_here(0)
+    grad_piece(0, 0)
     for dx in (1, 2):
         j = lax.rem(p.x + dx * s + 2 * NX, NX)
         remote(shard(j), shard(j), w_ss.at[0], w_rs.at[j], p.dev_x(1)).wait_recv()
+    back_rows(0)
+    relay_piece(0, 0)
+    grad_piece(0, 1)
+    pass_back(0)
+    weighted_here(1)
+    relay_piece(0, 1)
+    grad_piece(1, 0)
+    back_rows(1)
+    own_back = pltpu.make_async_copy(ws.at[p.own], rback.at[p.own], l_sem.at[3])
+    own_back.start()
+    relay_piece(1, 0)
+    grad_piece(1, 1)
+    pass_back(1)
     for c in early:
         c.wait_send()
-    home = peers(p, lambda c: 4 * c - 2)
-    k = 0
-    for dy in (2, 1, -1, 0):
-        yy = lax.rem(p.y + dy + NY, NY)
-        for e in range(held):
-            x_rows = xs[e, pl.ds(pl.multiple_of(yy * 256, 256), 256)]
-            got = lax.dot_general(
-                x_rows, wf[e], (((1,), (1,)), ((), ())), preferred_element_type=F32
-            )
-            ws[pl.ds(yy * 8, 8), e * CAP : (e + 1) * CAP] = got.astype(BF).reshape(8, CAP, hid)
-        for dev, dy2 in home:
-            if dy2 == dy:
-                start(
-                    remote(
-                        ws.at[dev["expert"]], rback.at[p.own], d_ss.at[k], d_rs.at[p.own], dev
-                    ),
-                    late,
-                )
-                k += 1
-    own_back = pltpu.make_async_copy(ws.at[p.own], rback.at[p.own], l_sem.at[3])
-    own_back.start()
 
     keep = rows // 2
+
+    def to_z(src, dst, k, e, h):
+        cols = pl.ds(h * piece, piece)
+        c = remote(
+            src.at[e, :, cols], dst.at[e, :, cols], z_ss.at[k, e, h], z_rs.at[k, e, h],
+            p.dev(0, 2 * s, core),
+        )
+        start(c, late)
+
+    def from_z(dst, k, e, h):
+        a = dst.at[e, :, pl.ds(h * piece, piece)]
+        remote(a, a, z_ss.at[k, e, h], z_rs.at[k, e, h], p.dev(0, 2 * s, core)).wait_recv()
+
+    def pass_z(e, h):
+        from_z(ez_t, 0, e, h)
+        to_z(ez_t, ez_r, 1, e, h)
 
     def reduce_piece(e, h):
         cols = pl.ds(h * piece, piece)
-        for k in range(3):
-            a = rg.at[k, e, :, cols]
-            remote(a, a, e_ss.at[e, h, k], e_rs.at[e, h, k], p.dev_x(1)).wait_recv()
+        from_x(e, h, 1)
+        from_x(e, h, 2)
 
         def total(r):
             at_r = pl.ds(pl.multiple_of(r * keep, keep), keep)
             t = own_g[e, at_r, cols]
-            for k in range(3):
+            for k in (1, 2):
                 t += rg[k, e, at_r, cols].astype(F32)
             return t
 
         ez_s[e, :, cols] = total(1 - p.half).astype(BF)
         gs_ref[e, :, cols] = total(p.half)
-        start(
-            remote(
-                ez_s.at[e, :, cols], ez_r.at[e, :, cols], z_ss.at[e, h], z_rs.at[e, h],
-                {"replica": 1 - p.half},
-            ),
-            late,
-        )
+        to_z(ez_s, ez_t, 0, e, h)
 
     reduce_piece(0, 0)
+    relay_piece(1, 1)
     reduce_piece(0, 1)
+    pass_z(0, 0)
+    reduce_piece(1, 0)
+    pass_z(0, 1)
 
     own_back.wait()
-    for dc in (0, 1):
-        c2 = core if dc == 0 else 1 - core
-        for dy in range(NY):
-            for dz in range(NZL):
-                if dc == 0 and dy == 0 and dz == 0:
-                    continue
-                j = p.slot(dy, dz, c2)
-                remote(
-                    rback.at[j], rback.at[j], d_ss.at[0], d_rs.at[j], p.dev(1, 0, core)
-                ).wait_recv()
-
-    named_c = ids_c_ref[...] == lax.broadcasted_iota(jnp.int32, (routes, experts), 1)
-    named_c = jnp.where(named_c, 1.0, 0.0).astype(BF)
+    for j in others():
+        for e in range(held):
+            a = of_expert(rback, j, e)
+            remote(a, a, d_ss.at[e, 0], d_rs.at[e, j], p.dev(1, 0, core)).wait_recv()
+
+    tk = step // top
+    sub = lax.broadcasted_iota(jnp.int32, (step, tokens), 0) // top
+    lane = lax.broadcasted_iota(jnp.int32, (step, tokens), 1)
 
     def join(i, _):
         r = pl.ds(pl.multiple_of(i * step, step), step)
-        here = lax.broadcasted_iota(jnp.int32, (step, routes), 0) + i * step
-        older = (lax.broadcasted_iota(jnp.int32, (step, routes), 1) < here).astype(F32)
-        rank = jnp.dot(older.astype(BF), named_c, preferred_element_type=F32)
-        mine = ids_c_ref[r] == lax.broadcasted_iota(jnp.int32, (step, experts), 1)
-        rank = jnp.sum(jnp.where(mine, rank, 0.0), axis=1, keepdims=True)
-        slot_c = ids_c_ref[r] * CAP + rank.astype(jnp.int32)
-        pick = slot_c == lax.broadcasted_iota(jnp.int32, (step, groups * slots), 1)
+        here = sub + i * tk == lane
+
+        def column(rows):
+            wide = jnp.broadcast_to(rows[None], (tk, top, tokens)).reshape(step, tokens)
+            return jnp.sum(jnp.where(here, wide, jnp.zeros_like(wide)), axis=1, keepdims=True)
+
+        pick = column(slot_t) == lax.broadcasted_iota(jnp.int32, (step, groups * slots), 1)
         got = jnp.dot(
             pick.astype(F32).astype(BF),
             rback[...].reshape(groups * slots, hid),
             preferred_element_type=F32,
         )
-        hg_ref[r] = (gate_ref[r] * got).astype(BF)
-        gg_ref[r] = jnp.sum(hid_ref[r].astype(F32) * got, axis=1, keepdims=True)
+        hg_ref[r] = (column(gate_ref[...]) * got).astype(BF)
+        dots = jnp.sum(hid_ref[r].astype(F32) * got, axis=1, keepdims=True)
+        gg_ref[...] += jnp.sum(
+            jnp.where(here, dots, 0.0).reshape(tk, top, tokens), axis=0
+        )
         return 0
 
+    gg_ref[...] = jnp.zeros_like(gg_ref)
     lax.fori_loop(0, routes // step, join, 0)
 
-    reduce_piece(1, 0)
+    pass_z(1, 0)
     reduce_piece(1, 1)
+    pass_z(1, 1)
     for e in range(held):
         for h in (0, 1):
             cols = pl.ds(h * piece, piece)
-            a = ez_r.at[e, :, cols]
-            remote(a, a, z_ss.at[e, h], z_rs.at[e, h], p.dev_x(1)).wait_recv()
+            from_z(ez_r, 1, e, h)
             gs_ref[e, :, cols] += ez_r[e, :, cols].astype(F32)
     for c in late:
         c.wait_send()
 
 
-def whole(dy, ids, ids_t, hidden, gate, ids_c, wq, we):
+def whole(dy, ids_t, hidden, gate_t, wq, we_t):
     tokens, width = dy.shape
     held, rows, _ = wq.shape
     routes, hid = hidden.shape
@@ -430,10 +552,10 @@
         whole_kernel,
         out_shape=(
             jax.ShapeDtypeStruct((routes, hid), BF),
-            jax.ShapeDtypeStruct((routes, 1), F32),
+            jax.ShapeDtypeStruct(gate_t.shape, F32),
             jax.ShapeDtypeStruct((held, rows // 2, width), F32),
         ),
-        in_specs=[VMEM] * 8,
+        in_specs=[VMEM] * 6,
         out_specs=(VMEM,) * 3,
         scratch_shapes=[
             vm((groups * tokens, width), BF),
@@ -446,19 +568,22 @@
             vm((held, rows, width), F32),
             vm((NX - 1, held, rows, width), BF),
             vm((groups, slots, hid), BF),
+            vm((2 * NZL, slots, hid), BF),
+            vm((2 * NZL, slots, hid), BF),
+            vm((held, rows // 2, width), BF),
             vm((held, rows // 2, width), BF),
             vm((held, rows // 2, width), BF),
             vm((held, groups, tokens), F32),
             vm((hid, 256), F32),
             dma((2, 15)), dma((2, 32)), dma((16,)), dma((32,)), dma((31,)), dma((32,)),
-            dma((31,)), dma((32,)), dma((3,)), dma((4,)), dma((31,)), dma((32,)),
-            dma((2, 2, 3)), dma((2, 2, 3)), dma((2, 2)), dma((2, 2)), dma((4,)),
+            dma((held, 32)), dma((held, 32)), dma((3,)), dma((4,)), dma((held, 32)), dma((held, 32)),
+            dma((2, 2, 3)), dma((2, 2, 3)), dma((2, held)), dma((2, 2, 2)), dma((2, 2, 2)), dma((4,)),
         ],
         compiler_params=pltpu.CompilerParams(
-            has_side_effects=True, vmem_limit_bytes=67043328
+            has_side_effects=True, vmem_limit_bytes=67043328, collective_id=0
         ),
         name="whole",
-    )(dy, ids, ids_t, hidden, gate, ids_c, wq, we)
+    )(dy, ids_t, hidden, gate_t, wq, we_t)
 
 
 def body(
@@ -468,23 +593,20 @@
     hid = hidden_saved.shape[2]
     routes = tokens * top
 
-    ids = expert_ids.reshape(1, routes)
     hidden_grad, gate_grad, gradient = whole(
         out_grad,
-        ids,
         expert_ids.T,
         hidden_saved.reshape(routes, hid),
-        gate_probs.reshape(routes, 1),
-        expert_ids.reshape(routes, 1),
+        gate_probs.T,
         weight_q,
-        weight_exp,
+        weight_exp.transpose(0, 2, 1),
     )
     first = 0.9 * moment1.astype(F32) + 0.1 * gradient
     second = 0.95 * moment2.astype(F32) + 0.05 * gradient * gradient
     update = first / (1.0 - 0.9**20) / (jnp.sqrt(second / (1.0 - 0.95**20)) + 1e-08) + 0.1 * master
     return (
         hidden_grad.reshape(tokens, top, hid),
-        gate_grad.reshape(tokens, top),
+        gate_grad.T,
         master - 0.001 * update,
         first.astype(BF),
         second.astype(BF),

time: 233 us -> 207 us (0.89)
  the two profiles are of different devices: /device:TPU:65 before, /device:TPU:32 now
where the time goes in v3:
time: 207 us
  Pallas kernels  199 us (96%)
  other arithmetic  5.92 us (3%)
    pallas_call x1, Pallas kernels, whole(): pl.pallas_call(whole_kernel, out_shape=(jax.ShapeDtypeStruct((routes, hid...  199 us
    convert_element_type x1, other arithmetic, body(): second.astype(BF)  5.92 us

profile of v3, /device:TPU:32, one launch (start us, length us, event | category | flops | bytes accessed | tf_op | source)
XLA Modules:
  0.0 207.2 jit_solution(9708722887746094381)
XLA Ops:
  0.6 198.9 %whole.1 = (bf16[1024,768]{1,0:T(8,128)(2,1)}, f32[8,128]{1,0:T(8,128)}, f32[2,96,2048]{2,1,0:T(8,128)}) custom-call(bf16[128,2048]{1,0:T(8,128)(2,1)} %dy_ref.1, s32[8,128]{1,0:T(8,128)} %bitcast.9, bf16[1024,768]{1,0:T(8,128)(2,1)} %bitcast.6, f32[8,128]{1,0:T(8,128)} %bitcast.10, bf16[2,192,2048]{2,1,0:T(8,128)(2,1)} %wq_ref.1, s32[2,16,192]{2,1,0:T(8,128)} %bitcast.8), custom_call_target="tpu_custom_call" | custom-call | tf_op jit(solution)/shard_map/whole/pallas_call | solution.py:551
  199.6 0.0 copy-start
  199.6 5.9 %fusion.2 = (bf16[2,96,2048]{2,1,0:T(8,128)(2,1)}, f32[2,96,2048]{2,1,0:T(8,128)}, bf16[2,96,2048]{2,1,0:T(8,128)(2,1)}) fusion(f32[2,96,2048]{2,1,0:T(8,128)} %get-tuple-element.10, bf16[2,96,2048]{2,1,0:T(8,128)(2,1)} %param.17, f32[2,96,2048]{2,1,0:T(8,128)} %param.15, bf16[2,96,2048]{2,1,0:T(8,128)(2,1)} %param.16), kind=kLoop, calls=%fused_computation.5 | loop fusion | flops 7471104 | bytes 7864320 | tf_op jit(solution)/shard_map/convert_element_type | solution.py:612
  205.5 0.0 copy-done
  205.5 0.0 copy-start.1
  205.5 1.1 copy.16
  206.6 0.0 copy-done.1
  206.6 0.6 copy.17
Async XLA Ops:
  199.6 5.9 %copy-start = (bf16[1024,768]{1,0:T(8,128)(2,1)S(1)}, bf16[1024,768]{1,0:T(8,128)(2,1)}, u32[]{:S(2)}) copy-start(bf16[1024,768]{1,0:T(8,128)(2,1)} %get-tuple-element.8) | copy-start | bytes 4718596
  205.5 1.1 copy-start.1

commit v4 on v3

--- a/solution.py
+++ b/solution.py
@@ -8,6 +8,12 @@
 MESH = pl.DeviceIdType.MESH
 NY, NZ, NZL, NX = 4, 8, 4, 4
 CAP = 32
+NP = 4
+ORDER = (
+    "V W0 g0", "g1 B0 O0", "r0 g2 r1", "g3 R0 P0", "W1 r2 g4", "R1 Z0 B1",
+    "O1 r3 g5", "R2 Z1 r4", "g6 R3 Z2", "r5 g7 R4", "Z3 P1 r6", "R5 Z4 r7",
+    "R6 Z5 R7", "Z6 Z7 D", "C04 F0 F1", "F2 F3 F4", "F5 F6 F7",
+)
 F32, BF = jnp.float32, jnp.bfloat16
 ANY = pl.BlockSpec(memory_space=pl.ANY)
 VMEM = pl.BlockSpec(memory_space=pltpu.VMEM)
@@ -271,7 +277,6 @@
             wait_dy(b, h)
             send_dy(part(b, h), b, h, p.dev(*at(h, 0, s), core))
     send_rows(1)
-    pass_rows(b_via, rw, 1, 0, b_ss, b_rs, lambda c: 2 * s, row_sends[1])
 
     back_x = lax.rem(p.x - s + NX, NX)
     remote(shard(back_x), shard(back_x), w_ss.at[2], w_rs.at[back_x], p.dev_x(s)).wait_recv()
@@ -341,6 +346,7 @@
     own_stage(1)
     sib_stage(0)
     own_stage(2)
+    pass_rows(b_via, rw, 1, 0, b_ss, b_rs, lambda c: 2 * s, row_sends[1])
     sib_stage(1)
     own_stage(3)
     sib_stage(2)
@@ -359,7 +365,7 @@
                         yield p.slot(dy, dz, c2)
 
     chunk = groups * CAP // 4
-    piece = width // 2
+    piece = width // NP
     nt = 256
     late = []
 
@@ -407,11 +413,18 @@
         rdy[r, cols] = (rdy[r, cols].astype(F32) + rg[0, e, :, cols].astype(F32)).astype(BF)
         to_x(e, h, 2, p.x + s, s)
 
+    back_at = held * hid
+
+    def back_of(e, j, n):
+        at_j = pl.multiple_of(back_at + e * groups * CAP + j * CAP, CAP)
+        return rdy.at[pl.ds(at_j, n * CAP), pl.ds(0, hid)]
+
     def back_tile(e, dy):
         yy = lax.rem(p.y + dy + NY, NY)
         x_rows = xs[e, pl.ds(pl.multiple_of(yy * 256, 256), 256)]
         got = lax.dot_general(x_rows, wf[e], (((1,), (1,)), ((), ())), preferred_element_type=F32)
-        ws[pl.ds(yy * 8, 8), e * CAP : (e + 1) * CAP] = got.astype(BF).reshape(8, CAP, hid)
+        to = pl.multiple_of(back_at + e * groups * CAP + yy * 256, 256)
+        rdy[pl.ds(to, 256), :hid] = got.astype(BF)
 
     home = peers(p, lambda c: 4 * c - 2)
 
@@ -419,38 +432,23 @@
         for dy in (2, 1, -1, 0):
             back_tile(e, dy)
             if dy == 2:
-                far = far_rows(ws, e, p.y + 2)
-                via = d_via.at[:, pl.ds(e * CAP, CAP)]
-                c = remote(far, via, d_ss.at[e, 31], v_rs.at[1, e], p.dev(s, 0, core))
+                far = back_of(e, lax.rem(p.y + 2, NY) * 2 * NZL, 2 * NZL)
+                c = remote(far, d_via.at[e], d_ss.at[e, 31], v_rs.at[1, e], p.dev(s, 0, core))
                 start(c, late)
             for k, (dev, dy2) in enumerate(home):
                 if dy2 == dy:
-                    src, dst = of_expert(ws, dev["expert"], e), of_expert(rback, p.own, e)
+                    src, dst = back_of(e, dev["expert"], 1), of_expert(rback, p.own, e)
                     start(remote(src, dst, d_ss.at[e, k], d_rs.at[e, p.own], dev), late)
 
     def pass_back(e):
-        pass_rows(d_via, rback, e, 1, d_ss, d_rs, lambda c: 4 * c - 2, late)
-
-    weighted_here(0)
-    grad_piece(0, 0)
-    for dx in (1, 2):
-        j = lax.rem(p.x + dx * s + 2 * NX, NX)
-        remote(shard(j), shard(j), w_ss.at[0], w_rs.at[j], p.dev_x(1)).wait_recv()
-    back_rows(0)
-    relay_piece(0, 0)
-    grad_piece(0, 1)
-    pass_back(0)
-    weighted_here(1)
-    relay_piece(0, 1)
-    grad_piece(1, 0)
-    back_rows(1)
-    own_back = pltpu.make_async_copy(ws.at[p.own], rback.at[p.own], l_sem.at[3])
-    own_back.start()
-    relay_piece(1, 0)
-    grad_piece(1, 1)
-    pass_back(1)
-    for c in early:
-        c.wait_send()
+        blk = d_via.at[e]
+        remote(blk, blk, d_ss.at[e, 31], v_rs.at[1, e], p.dev(s, 0, core)).wait_recv()
+        origin = p.slot(-s, 0, core)
+        for i, dev in enumerate(far_row(p, s, lambda c: 4 * c - 2)):
+            j = lax.rem(dev["expert"], 2 * NZL)
+            src = d_via.at[e, pl.ds(pl.multiple_of(j * CAP, CAP), CAP)]
+            dst = of_expert(rback, origin, e)
+            start(remote(src, dst, d_ss.at[e, 23 + i], d_rs.at[e, origin], dev), late)
 
     keep = rows // 2
 
@@ -485,19 +483,6 @@
         ez_s[e, :, cols] = total(1 - p.half).astype(BF)
         gs_ref[e, :, cols] = total(p.half)
         to_z(ez_s, ez_t, 0, e, h)
-
-    reduce_piece(0, 0)
-    relay_piece(1, 1)
-    reduce_piece(0, 1)
-    pass_z(0, 0)
-    reduce_piece(1, 0)
-    pass_z(0, 1)
-
-    own_back.wait()
-    for j in others():
-        for e in range(held):
-            a = of_expert(rback, j, e)
-            remote(a, a, d_ss.at[e, 0], d_rs.at[e, j], p.dev(1, 0, core)).wait_recv()
 
     tk = step // top
     sub = lax.broadcasted_iota(jnp.int32, (step, tokens), 0) // top
@@ -524,18 +509,53 @@
         )
         return 0
 
+    def joins(lo, hi):
+        lax.fori_loop(lo, hi, join, 0)
+
+    def whole_weights():
+        for dx in (1, 2):
+            j = lax.rem(p.x + dx * s + 2 * NX, NX)
+            remote(shard(j), shard(j), w_ss.at[0], w_rs.at[j], p.dev_x(1)).wait_recv()
+
+    def returned():
+        for c in own_back:
+            c.wait()
+        for j in others():
+            for e in range(held):
+                a = of_expert(rback, j, e)
+                remote(a, a, d_ss.at[e, 0], d_rs.at[e, j], p.dev(1, 0, core)).wait_recv()
+
+    def finish(e, h):
+        cols = pl.ds(h * piece, piece)
+        from_z(ez_r, 1, e, h)
+        gs_ref[e, :, cols] += ez_r[e, :, cols].astype(F32)
+
     gg_ref[...] = jnp.zeros_like(gg_ref)
-    lax.fori_loop(0, routes // step, join, 0)
-
-    pass_z(1, 0)
-    reduce_piece(1, 1)
-    pass_z(1, 1)
-    for e in range(held):
-        for h in (0, 1):
-            cols = pl.ds(h * piece, piece)
-            from_z(ez_r, 1, e, h)
-            gs_ref[e, :, cols] += ez_r[e, :, cols].astype(F32)
-    for c in late:
+    own_back = [
+        pltpu.make_async_copy(back_of(e, p.own, 1), of_expert(rback, p.own, e), l_sem.at[2 + e])
+        for e in range(held)
+    ]
+    steps = {
+        "g": grad_piece, "r": relay_piece, "R": reduce_piece, "Z": pass_z, "F": finish,
+    }
+    for word in " ".join(ORDER).split():
+        if word[0] in steps:
+            steps[word[0]](int(word[1:]) // NP, int(word[1:]) % NP)
+        elif word[0] == "W":
+            weighted_here(int(word[1]))
+        elif word == "V":
+            whole_weights()
+        elif word[0] == "B":
+            back_rows(int(word[1]))
+        elif word[0] == "P":
+            pass_back(int(word[1]))
+        elif word[0] == "O":
+            own_back[int(word[1])].start()
+        elif word == "D":
+            returned()
+        elif word[0] == "C":
+            joins(int(word[1]), int(word[2]))
+    for c in early + late:
         c.wait_send()
 
 
@@ -569,7 +589,7 @@
             vm((NX - 1, held, rows, width), BF),
             vm((groups, slots, hid), BF),
             vm((2 * NZL, slots, hid), BF),
-            vm((2 * NZL, slots, hid), BF),
+            vm((held, 2 * NZL * CAP, hid), BF),
             vm((held, rows // 2, width), BF),
             vm((held, rows // 2, width), BF),
             vm((held, rows // 2, width), BF),
@@ -577,7 +597,7 @@
             vm((hid, 256), F32),
             dma((2, 15)), dma((2, 32)), dma((16,)), dma((32,)), dma((31,)), dma((32,)),
             dma((held, 32)), dma((held, 32)), dma((3,)), dma((4,)), dma((held, 32)), dma((held, 32)),
-            dma((2, 2, 3)), dma((2, 2, 3)), dma((2, held)), dma((2, 2, 2)), dma((2, 2, 2)), dma((4,)),
+            dma((held, NP, 3)), dma((held, NP, 3)), dma((2, held)), dma((2, held, NP)), dma((2, held, NP)), dma((4,)),
         ],
         compiler_params=pltpu.CompilerParams(
             has_side_effects=True, vmem_limit_bytes=67043328, collective_id=0

time: 207 us -> 187 us (0.903)
  Pallas kernels: 199 us -> 179 us
    pallas_call x1, Pallas kernels: 199 us -> 179 us  [whole(): pl.pallas_call(whole_kernel, out_shape=(jax.ShapeDtypeStruct((routes, hid...]
where the time goes in v4:
time: 187 us
  Pallas kernels  179 us (96%)
  other arithmetic  5.92 us (3%)
    pallas_call x1, Pallas kernels, whole(): pl.pallas_call(whole_kernel, out_shape=(jax.ShapeDtypeStruct((routes, hid...  179 us
    convert_element_type x1, other arithmetic, body(): second.astype(BF)  5.92 us

profile of v4, /device:TPU:32, one launch (start us, length us, event | category | flops | bytes accessed | tf_op | source)
XLA Modules:
  0.0 187.3 jit_solution(15153181731230850039)
XLA Ops:
  0.6 179.0 %whole.1 = (bf16[1024,768]{1,0:T(8,128)(2,1)}, f32[8,128]{1,0:T(8,128)}, f32[2,96,2048]{2,1,0:T(8,128)}) custom-call(bf16[128,2048]{1,0:T(8,128)(2,1)} %dy_ref.1, s32[8,128]{1,0:T(8,128)} %bitcast.9, bf16[1024,768]{1,0:T(8,128)(2,1)} %bitcast.6, f32[8,128]{1,0:T(8,128)} %bitcast.10, bf16[2,192,2048]{2,1,0:T(8,128)(2,1)} %wq_ref.1, s32[2,16,192]{2,1,0:T(8,128)} %bitcast.8), custom_call_target="tpu_custom_call" | custom-call | tf_op jit(solution)/shard_map/whole/pallas_call | solution.py:571
  179.6 0.0 copy-start
  179.6 5.9 %fusion.2 = (bf16[2,96,2048]{2,1,0:T(8,128)(2,1)}, f32[2,96,2048]{2,1,0:T(8,128)}, bf16[2,96,2048]{2,1,0:T(8,128)(2,1)}) fusion(f32[2,96,2048]{2,1,0:T(8,128)} %get-tuple-element.10, bf16[2,96,2048]{2,1,0:T(8,128)(2,1)} %param.17, f32[2,96,2048]{2,1,0:T(8,128)} %param.15, bf16[2,96,2048]{2,1,0:T(8,128)(2,1)} %param.16), kind=kLoop, calls=%fused_computation.5 | loop fusion | flops 7471104 | bytes 7864320 | tf_op jit(solution)/shard_map/convert_element_type | solution.py:632
  185.5 0.0 copy-done
  185.5 0.0 copy-start.1
  185.5 1.1 copy.16
  186.7 0.0 copy-done.1
  186.7 0.6 copy.17
Async XLA Ops:
  179.6 5.9 %copy-start = (bf16[1024,768]{1,0:T(8,128)(2,1)S(1)}, bf16[1024,768]{1,0:T(8,128)(2,1)}, u32[]{:S(2)}) copy-start(bf16[1024,768]{1,0:T(8,128)(2,1)} %get-tuple-element.8) | copy-start | bytes 4718596
  185.5 1.1 copy-start.1

commit v5 on v4

--- a/solution.py
+++ b/solution.py
@@ -10,9 +10,9 @@
 CAP = 32
 NP = 4
 ORDER = (
-    "V W0 g0", "g1 B0 O0", "r0 g2 r1", "g3 R0 P0", "W1 r2 g4", "R1 Z0 B1",
-    "O1 r3 g5", "R2 Z1 r4", "g6 R3 Z2", "r5 g7 R4", "Z3 P1 r6", "R5 Z4 r7",
-    "R6 Z5 R7", "Z6 Z7 D", "C04 F0 F1", "F2 F3 F4", "F5 F6 F7",
+    "V W0 g0", "g1 B0 O0", "r0 g2 r1", "g3 R0 P0", "W1 r2 g4", "R1 B1 O1",
+    "r3 g5 R2", "Z0 r4 g6", "R3 Z1 r5", "g7 R4 Z2", "P1 r6 R5", "Z3 r7 R6",
+    "Z4 R7 Z5", "Z6 D C02", "Z7 C24 F0", "F1 F2 F3", "F4 F5 F6", "F7",
 )
 F32, BF = jnp.float32, jnp.bfloat16
 ANY = pl.BlockSpec(memory_space=pl.ANY)
@@ -88,9 +88,9 @@
 
 
 def whole_kernel(
-    dy_ref, ids_t_ref, hid_ref, gate_ref, wq_ref, we_ref,
+    dy_ref, ids_t_ref, hid_in, gate_ref, wq_in, we_ref,
     hg_ref, gg_ref, gs_ref,
-    rdy, rids, rw, ws, wf, xs, wt, own_g, rg, rback, b_via, d_via, ez_s, ez_t, ez_r, code, g_tile,
+    rdy, rids, rw, ws, wf, xs, wt, own_g, rg, rback, b_via, d_via, ez_s, ez_t, ez_r, code, g_tile, hid_ref, wq_ref,
     dy_ss, dy_rs, sib_ss, sib_rs, id_ss, id_rs, b_ss, b_rs, w_ss, w_rs, d_ss, d_rs, e_ss, e_rs,
     v_rs, z_ss, z_rs, l_sem,
 ):
@@ -135,6 +135,13 @@
     def wait_sib(slot):
         blk = block(slot)
         remote(blk, blk, sib_ss.at[0], sib_rs.at[slot], p.dev(0, 0, 1 - core)).wait_recv()
+
+    loads = [
+        pltpu.make_async_copy(wq_in, wq_ref, l_sem.at[4]),
+        pltpu.make_async_copy(hid_in, hid_ref, l_sem.at[5]),
+    ]
+    for c in loads:
+        c.start()
 
     gate = pltpu.get_barrier_semaphore()
     near = [dev for dev, _ in peers(p, lambda c: 2 * s)] + far_row(p, 2, lambda c: 2 * s)
@@ -169,6 +176,7 @@
 
     mine_w = pl.ds(pl.multiple_of(p.x * rows, rows), rows)
     qb = width // we_ref.shape[1]
+    loads[0].wait()
     for e in range(held):
         blocks = we_ref.shape[1]
         same = lax.broadcasted_iota(jnp.int32, (blocks, blocks), 0) == lax.broadcasted_iota(
@@ -209,6 +217,7 @@
     slot_row = jnp.sum(
         jnp.where(mine_k, both[:top] * CAP + both[top:], 0.0), axis=0, keepdims=True
     ).astype(jnp.int32)
+    loads[1].wait()
     hg_ref[...] = (spread(gate_ref[...]) * hid_ref[...].astype(F32)).astype(BF)
 
     for i, dx in enumerate((1, -1)):
@@ -575,7 +584,7 @@
             jax.ShapeDtypeStruct(gate_t.shape, F32),
             jax.ShapeDtypeStruct((held, rows // 2, width), F32),
         ),
-        in_specs=[VMEM] * 6,
+        in_specs=[VMEM, VMEM, ANY, VMEM, ANY, VMEM],
         out_specs=(VMEM,) * 3,
         scratch_shapes=[
             vm((groups * tokens, width), BF),
@@ -595,9 +604,11 @@
             vm((held, rows // 2, width), BF),
             vm((held, groups, tokens), F32),
             vm((hid, 256), F32),
+            vm((routes, hid), BF),
+            vm(wq.shape, BF),
             dma((2, 15)), dma((2, 32)), dma((16,)), dma((32,)), dma((31,)), dma((32,)),
             dma((held, 32)), dma((held, 32)), dma((3,)), dma((4,)), dma((held, 32)), dma((held, 32)),
-            dma((held, NP, 3)), dma((held, NP, 3)), dma((2, held)), dma((2, held, NP)), dma((2, held, NP)), dma((4,)),
+            dma((held, NP, 3)), dma((held, NP, 3)), dma((2, held)), dma((2, held, NP)), dma((2, held, NP)), dma((6,)),
         ],
         compiler_params=pltpu.CompilerParams(
             has_side_effects=True, vmem_limit_bytes=67043328, collective_id=0

time: 187 us -> 184 us (0.984); the launches traced: 187 us -> 182 us
  Pallas kernels: 179 us -> 174 us
    pallas_call x1, Pallas kernels: 179 us -> 174 us  [whole(): pl.pallas_call(whole_kernel, out_shape=(jax.ShapeDtypeStruct((routes, hid...]
where the time goes in v5:
time: 184 us; the launch traced here: 182 us
  Pallas kernels  174 us (95%)
  other arithmetic  5.92 us (3%)
    pallas_call x1, Pallas kernels, whole(): pl.pallas_call(whole_kernel, out_shape=(jax.ShapeDtypeStruct((routes, hid...  174 us
    convert_element_type x1, other arithmetic, body(): second.astype(BF)  5.92 us

profile of v5, /device:TPU:32, one launch (start us, length us, event | category | flops | bytes accessed | tf_op | source)
XLA Modules:
  0.0 182.1 jit_solution(5560803664459542384)
XLA Ops:
  0.6 173.8 %whole.1 = (bf16[1024,768]{1,0:T(8,128)(2,1)}, f32[8,128]{1,0:T(8,128)}, f32[2,96,2048]{2,1,0:T(8,128)}) custom-call(bf16[128,2048]{1,0:T(8,128)(2,1)} %dy_ref.1, s32[8,128]{1,0:T(8,128)} %bitcast.9, bf16[1024,768]{1,0:T(8,128)(2,1)} %bitcast.6, f32[8,128]{1,0:T(8,128)} %bitcast.10, bf16[2,192,2048]{2,1,0:T(8,128)(2,1)} %wq_in.1, s32[2,16,192]{2,1,0:T(8,128)} %bitcast.8), custom_call_target="tpu_custom_call" | custom-call | tf_op jit(solution)/shard_map/whole/pallas_call | solution.py:580
  174.4 0.0 copy-start
  174.5 5.9 %fusion.2 = (bf16[2,96,2048]{2,1,0:T(8,128)(2,1)}, f32[2,96,2048]{2,1,0:T(8,128)}, bf16[2,96,2048]{2,1,0:T(8,128)(2,1)}) fusion(f32[2,96,2048]{2,1,0:T(8,128)} %get-tuple-element.10, bf16[2,96,2048]{2,1,0:T(8,128)(2,1)} %param.17, f32[2,96,2048]{2,1,0:T(8,128)} %param.15, bf16[2,96,2048]{2,1,0:T(8,128)(2,1)} %param.16), kind=kLoop, calls=%fused_computation.5 | loop fusion | flops 7471104 | bytes 7864320 | tf_op jit(solution)/shard_map/convert_element_type | solution.py:643
  180.4 0.0 copy-done
  180.4 0.0 copy-start.1
  180.4 1.1 copy.16
  181.5 0.0 copy-done.1
  181.5 0.6 copy.17
Async XLA Ops:
  174.4 5.9 %copy-start = (bf16[1024,768]{1,0:T(8,128)(2,1)S(1)}, bf16[1024,768]{1,0:T(8,128)(2,1)}, u32[]{:S(2)}) copy-start(bf16[1024,768]{1,0:T(8,128)(2,1)} %get-tuple-element.8) | copy-start | bytes 4718596
  180.4 1.1 copy-start.1
